TPU v7x, 256 devices: a whole 4x4x8 slice. The times are simulated.
256 devices in a mesh: ctx: 4 (over x_hi, core), exp: 64 (over x_lo, z, y).
Axes of the slice: x: 4 (x_hi: 2, x_lo: 2; x = x_hi * 2 + x_lo), y: 4, z: 8, core: 2. Of those that a mesh axis runs over, the one named last changes fastest.
Arguments:
- tokens: bfloat16 [64, 512, 1024], P('exp', 'ctx'), may hold values from -300 to 300, as said below
- expert_ids: int32 [64, 512, 2], P('exp', 'ctx'), may hold values from 0 to 63, all different within a row; in each aligned block of 128 rows (0 to 127, 128 to 255, ..., all dimensions but the last counted through in order) at most 6 rows name the same one
- attn_gain: float32 [1024], replicated, may hold values from 0.1 to 1.9
- w_query: bfloat16 [1024, 1024], P('exp'), may hold values from -0.1875 to 0.1875
- w_kv: bfloat16 [1024, 256], P('exp'), may hold values from -0.1875 to 0.1875
- w_out: bfloat16 [1024, 1024], P('exp'), may hold values from -0.1875 to 0.1875
- moe_gain: float32 [1024], replicated, may hold values from 0.1 to 1.9
- router: bfloat16 [1024, 64], replicated, may hold values from -0.375 to 0.375
- w_gate: bfloat16 [64, 1024, 4096], P('exp', None, 'ctx'), may hold values from -0.1875 to 0.1875
- w_up: bfloat16 [64, 1024, 4096], P('exp', None, 'ctx'), may hold values from -0.1875 to 0.1875
- w_down: bfloat16 [64, 4096, 1024], P('exp', 'ctx'), may hold values from -0.1875 to 0.1875
Outputs:
- attention_out: bfloat16 [64, 512, 1024], P('exp', 'ctx')
- expert_mix: bfloat16 [64, 512, 1024], P('exp', 'ctx')
Inputs may be any that keep to these rules, and one draw needn't show every extreme that they name: `expert_ids`: each row names 2 different experts. In the rows of one device (aligned blocks of 128 positions) no expert is named more than 6 times, a bound that some block reaches in every draw. `tokens`: each token and each feature carries its own scale.
All inputs are finite; a program needn't handle non-finite values.
Results may differ from a plain program's by a relative error of at most 0.018.
Values may be sent and summed in bfloat16 or wider, within the bound.
A program may use at most 128 MiB of HBM per device.

v0:
```python
import jax
import jax.numpy as jnp
from jax import lax
from jax.sharding import PartitionSpec as P

HD = 128
TOP = 2


epsilon = 1e-06


def rms_scaled(values):
    return values * lax.rsqrt(jnp.mean(values * values, axis=-1, keepdims=True) + epsilon)


def body(
    tokens, expert_ids, attn_gain, w_query, w_kv, w_out, moe_gain, router, w_gate, w_up, w_down
):
    features = tokens.shape[-1]
    inputs = tokens.reshape(-1, features)
    tok_rows = inputs.shape[0]
    full_query, full_kv, full_out = (
        lax.all_gather(w_query, "exp", axis=0, tiled=True),
        lax.all_gather(w_kv, "exp", axis=0, tiled=True),
        lax.all_gather(w_out, "exp", axis=0, tiled=True),
    )
    floats = inputs.astype(jnp.float32)
    attn_in = (rms_scaled(floats) * attn_gain).astype(jnp.bfloat16)
    head_count = full_query.shape[1] // HD
    queries = jnp.dot(attn_in, full_query, preferred_element_type=jnp.float32).reshape(
        tok_rows, head_count, HD
    )
    queries = rms_scaled(queries).astype(jnp.bfloat16).reshape(tok_rows * head_count, HD)
    key_value = jnp.dot(attn_in, full_kv, preferred_element_type=jnp.float32)
    keys = rms_scaled(key_value[:, :HD]).astype(jnp.bfloat16)
    values = key_value[:, HD:].astype(jnp.bfloat16)
    score_scale = HD ** (-0.5)
    key_piece = lax.all_gather(keys, "ctx", axis=0, tiled=True)
    value_piece = lax.all_gather(values, "ctx", axis=0, tiled=True)
    scores = (
        lax.dot_general(
            queries, key_piece, (((1,), (1,)), ((), ())), preferred_element_type=jnp.float32
        )
        * score_scale
    )
    weights = jnp.exp(scores).astype(jnp.bfloat16)
    weighted = jnp.dot(weights, value_piece, preferred_element_type=jnp.float32)
    totals = jnp.sum(weights.astype(jnp.float32), axis=1)
    weighted, totals = (weighted, totals)
    context = (weighted / totals[:, None]).astype(jnp.bfloat16).reshape(tok_rows, head_count * HD)
    attention_out = jnp.dot(context, full_out, preferred_element_type=jnp.float32).astype(
        jnp.bfloat16
    )
    mixed_in = floats + attention_out.astype(jnp.float32)
    moe_in = (rms_scaled(mixed_in) * moe_gain).astype(jnp.bfloat16)
    experts = router.shape[1]
    logits = jnp.dot(moe_in, router, preferred_element_type=jnp.float32)
    pair_ids = expert_ids.reshape(tok_rows, TOP)
    match = pair_ids[:, :, None] == jnp.arange(experts)[None, None, :]
    chosen = jnp.sum(jnp.where(match, logits[:, None, :], 0.0), axis=2)
    first = jax.nn.sigmoid(chosen[:, 0] - chosen[:, 1])
    gates = jnp.stack([first, 1.0 - first], axis=1)
    counts = match.reshape(tok_rows * TOP, experts).astype(jnp.int32)
    earlier = jnp.cumsum(counts, axis=0) - counts
    slot = jnp.sum(earlier * counts, axis=1)
    capacity = max(2, 3 * tok_rows * TOP // (2 * experts))
    position = slot * experts + pair_ids.reshape(-1)
    buffer = (
        jnp.zeros((capacity * experts, features), jnp.bfloat16)
        .at[position]
        .set(jnp.repeat(moe_in, TOP, axis=0))
    )
    received = lax.all_to_all(
        buffer.reshape(capacity, experts, features), "exp", split_axis=1, concat_axis=0, tiled=True
    )
    gathered = lax.all_gather(received, "ctx", axis=0, tiled=True)
    gated = jnp.einsum("red,edf->ref", gathered, w_gate, preferred_element_type=jnp.float32)
    lifted = jnp.einsum("red,edf->ref", gathered, w_up, preferred_element_type=jnp.float32)
    hidden = (jax.nn.silu(gated) * lifted).astype(jnp.bfloat16)
    summed = lax.psum_scatter(
        jnp.einsum("ref,efd->red", hidden, w_down, preferred_element_type=jnp.float32).astype(
            jnp.bfloat16
        ),
        "ctx",
        scatter_dimension=0,
        tiled=True,
    )
    returned = lax.all_to_all(summed, "exp", split_axis=0, concat_axis=1, tiled=True)
    picked = returned.reshape(capacity * experts, features)[position].reshape(
        tok_rows, TOP, features
    )
    expert_mix = jnp.sum(gates[:, :, None] * picked.astype(jnp.float32), axis=1).astype(
        jnp.bfloat16
    )
    return (attention_out.reshape(tokens.shape), expert_mix.reshape(tokens.shape))


def solution(mesh):
    in_specs = (
        P("exp", "ctx", None),
        P("exp", "ctx", None),
        P(),
        P("exp", None),
        P("exp", None),
        P("exp", None),
        P(),
        P(),
        P("exp", None, "ctx"),
        P("exp", None, "ctx"),
        P("exp", "ctx", None),
    )
    out_specs = (P("exp", "ctx", None), P("exp", "ctx", None))
    return jax.shard_map(body, mesh=mesh, in_specs=in_specs, out_specs=out_specs, check_vma=False)
```

profile of v0, /device:TPU:1, one launch (start us, length us, event | category | flops | bytes accessed | tf_op | source)
XLA Modules:
  0.0 806.8 jit_solution(10431472635085726552)
XLA Ops:
  7.2 0.7 all-gather.4.cloned.1.call-update
  8.0 0.7 all-gather.6.cloned.1.call-update
  8.7 0.8 copy.51
  9.5 0.1 reshape_reshape.3
  9.6 0.1 eq.42
  9.8 0.1 eq.38
  9.9 0.6 reduce-window.6
  10.6 0.2 slice_reduce_fusion
  10.8 1.1 fusion.19
  11.9 137.2 %all_gather.19 = bf16[1024,256]{1,0:T(8,128)(2,1)S(1)} all-gather(bf16[16,256]{1,0:T(8,128)(2,1)} %param.15), channel_id=1, replica_groups=mesh['ctx'=4,'exp'=64] {'exp'}, dimensions={0}, use_global_device_ids=true | all-gather | bytes 532480 | tf_op jit(solution)/shard_map/all_gather | solution.py:25
  149.1 1.2 fusion.29
  150.3 33.4 %all_gather.21 = bf16[512,128]{1,0:T(8,128)(2,1)S(1)} all-gather(bf16[128,128]{1,0:T(8,128)(2,1)S(1)} %slice.36), channel_id=1, replica_groups=mesh['ctx'=4,'exp'=64] {'ctx'}, dimensions={0}, use_global_device_ids=true | all-gather | bytes 163840 | tf_op jit(solution)/shard_map/all_gather | solution.py:40
  183.9 6.9 all_gather.20
  191.0 79.1 %all-gather.4.cloned.1.call-done = bf16[1024,1024]{1,0:T(8,128)(2,1)} async-done(((bf16[16,1024]{1,0:T(8,128)(2,1)}), bf16[1024,1024]{1,0:T(8,128)(2,1)}) %all-gather.4.cloned.1.call-update) | async-done | bytes 2097168 | tf_op jit(solution)/shard_map/all_gather | solution.py:24
  270.1 4.0 copy.48
  274.1 2.5 multiply_reduce_fusion.2
  276.6 0.2 multiply_convert_fusion.1
  276.8 0.5 convert_reduce_fusion
  277.4 0.5 fusion.15
  277.9 0.1 reshape.158
  278.0 289.3 %all-gather.6.cloned.1.call-done = bf16[1024,1024]{1,0:T(8,128)(2,1)} async-done(((bf16[16,1024]{1,0:T(8,128)(2,1)}), bf16[1024,1024]{1,0:T(8,128)(2,1)}) %all-gather.6.cloned.1.call-update) | async-done | bytes 2097168 | tf_op jit(solution)/shard_map/all_gather | solution.py:26
  567.4 2.1 multiply_reduce_fusion.1
  569.5 0.7 copy-done.2
  570.2 0.1 multiply_convert_fusion
  570.3 0.3 broadcast_in_dim.19
  570.6 1.0 reshape.183
  571.6 2.4 scatter_custom_fusion
  574.0 0.4 copy.55
  574.5 24.6 %all_to_all.33 = bf16[6,64,1024]{2,0,1:T(8,128)(2,1)S(1)} all-to-all(bf16[6,64,1024]{2,0,1:T(8,128)(2,1)S(1)} %copy.55), channel_id=1, replica_groups=mesh['ctx'=4,'exp'=64] {'exp'}, dimensions={1} | all-to-all | bytes 1572864 | tf_op jit(solution)/shard_map/all_to_all | solution.py:74
  599.1 1.1 all_to_all.27
  600.2 0.2 reduce-scatter.2.cloned.1.call-start
  600.5 79.6 %all-gather.8.cloned.1.call-done = bf16[1536,1,1024]{2,0,1:T(8,128)(2,1)} async-done(((bf16[384,1,1024]{2,0,1:T(8,128)(2,1)}), bf16[1536,1,1024]{2,0,1:T(8,128)(2,1)}) %all-gather.8.cloned.1.call-update) | async-done | bytes 3145744 | tf_op jit(solution)/shard_map/all_gather | solution.py:77
  680.1 7.3 fusion.7
  687.3 11.7 %fusion.4 = bf16[1536,1,1024]{2,0,1:T(8,128)(2,1)} fusion(f32[1536,1024]{1,0:T(8,128)} %fusion.7, bf16[1536,1,1024]{2,0,1:T(8,128)(2,1)} %all-gather.8.cloned.1.call-done, bf16[1,1024,1024]{2,1,0:T(8,128)(2,1)} %param.21, bf16[1,1024,1024]{2,1,0:T(8,128)(2,1)} %param.20), kind=kOutput, calls=%fused_computation.10 | convolution fusion | flops 6453460992 | bytes 16777216 | tf_op jit(solution)/shard_map/ref,efd->red/dot_general | solution.py:82
  699.0 49.2 %reduce-scatter.2.cloned.1.call-done = bf16[384,1,1024]{2,0,1:T(8,128)(2,1)} async-done(((bf16[1536,1,1024]{2,0,1:T(8,128)(2,1)}), bf16[384,1,1024]{2,0,1:T(8,128)(2,1)}) %reduce-scatter.2.cloned.1.call-update) | async-done | bytes 786448 | tf_op jit(solution)/shard_map/reduce_scatter | solution.py:81
  748.2 0.5 broadcast.139
  748.7 2.4 reduce.3
  751.1 1.4 reshape.192
  752.5 10.4 %all-to-all-start.1 = ((bf16[64,2,3072]{2,1,0:T(2,128)(2,1)}), bf16[64,2,3072]{2,1,0:T(2,128)(2,1)S(1)}, u32[]{:S(2)}, u32[]{:S(2)}) async-start(bf16[64,2,3072]{2,1,0:T(2,128)(2,1)} %reshape.192), calls=%async_computation.2 | async-start | bytes 1572864 | tf_op jit(solution)/shard_map/all_to_all | solution.py:89
  763.0 0.2 fusion.42
  763.4 20.5 %all-to-all-done.1 = bf16[64,2,3072]{2,1,0:T(2,128)(2,1)S(1)} async-done(((bf16[64,2,3072]{2,1,0:T(2,128)(2,1)}), bf16[64,2,3072]{2,1,0:T(2,128)(2,1)S(1)}, u32[]{:S(2)}, u32[]{:S(2)}) %all-to-all-start.1) | async-done | bytes 786464 | tf_op jit(solution)/shard_map/all_to_all | solution.py:89
  783.9 2.0 reshape.193
  785.9 5.8 reduce.1
  791.6 1.2 all_to_all.29
  792.9 1.7 copy.57
  794.5 2.0 gather_fusion
  796.5 1.7 reshape.170
  798.2 2.1 multiply_reduce_fusion
  (36 shorter events, 0.7 us)
Async XLA Ops:
  7.2 672.9 %copy-start = (bf16[1,1024,1024]{2,1,0:T(8,128)(2,1)S(1)}, bf16[1,1024,1024]{2,1,0:T(8,128)(2,1)}, u32[]{:S(2)}) copy-start(bf16[1,1024,1024]{2,1,0:T(8,128)(2,1)} %param.19) | copy-start | bytes 6291460
  7.2 262.9 %all-gather.4.cloned.1.call-start = ((), (), s32[]{:S(2)}) async-start(), calls=%async_computation.3 | async-start | bytes 2129920 | tf_op jit(solution)/shard_map/all_gather | solution.py:24
  7.9 559.4 %all-gather.6.cloned.1.call-start = ((), (), s32[]{:S(2)}) async-start(), calls=%async_computation.4 | async-start | bytes 2129920 | tf_op jit(solution)/shard_map/all_gather | solution.py:26
  8.7 671.4 %all-gather.8.cloned.1.call-start = ((), (), s32[]{:S(2)}) async-start(), calls=%async_computation.5 | async-start | bytes 3932160 | tf_op jit(solution)/shard_map/all_gather | solution.py:77
  270.1 4.0 copy-start.1
  270.1 4.0 copy-start.4
  277.9 292.3 %copy-start.5 = (f32[1024]{0:T(1024)S(1)}, f32[1024]{0:T(1024)}, u32[]{:S(2)}) copy-start(f32[1024]{0:T(1024)} %param.17) | copy-start | bytes 12292
  569.5 0.7 copy-start.2
  600.2 148.0 %reduce-scatter.2.cloned.1.call-start = ((), (), s32[]{:S(2)}) async-start(), calls=%async_computation.6 | async-start | bytes 3932160 | tf_op jit(solution)/shard_map/reduce_scatter | solution.py:81
  748.7 14.2 %copy-start.3 = (bf16[1024,64]{0,1:T(8,128)(2,1)S(1)}, bf16[1024,64]{0,1:T(8,128)(2,1)}, u32[]{:S(2)}) copy-start(bf16[1024,64]{0,1:T(8,128)(2,1)} %param.18) | copy-start | bytes 393220
  751.1 12.1 %copy-start.6 = (s32[1,128,2]{1,2,0:T(2,128)S(1)}, s32[1,128,2]{1,2,0:T(2,128)}, u32[]{:S(2)}) copy-start(s32[1,128,2]{1,2,0:T(2,128)} %param.12) | copy-start | bytes 3076
  752.5 31.4 %all-to-all-start.1 = ((bf16[64,2,3072]{2,1,0:T(2,128)(2,1)}), bf16[64,2,3072]{2,1,0:T(2,128)(2,1)S(1)}, u32[]{:S(2)}, u32[]{:S(2)}) async-start(bf16[64,2,3072]{2,1,0:T(2,128)(2,1)} %reshape.192), calls=%async_computation.2 | async-start | bytes 1572864 | tf_op jit(solution)/shard_map/all_to_all | solution.py:89
Sparse Core Ops, SparseCore 0:
  9.8 260.2 all-gather.3
  271.9 295.4 all-gather.5
  600.4 79.6 all-gather.7
  699.1 49.0 reduce-scatter.1
where the time goes:
time: 809 us; the launch traced here: 807 us
  waiting for transfers between devices  519 us (64%)
  blocking collectives  202 us (25%)
  matrix products  26.1 us (3%)
  local copies, waits for them, and re-layouts  22 us (3%)
  between operations  14 us (2%)
  other arithmetic  12.7 us (2%)
  starting transfers between devices  10.8 us (1%)
    all_gather x1, waiting for transfers between devices, body(): lax.all_gather(w_out, 'exp', axis=0, tiled=True)  289 us
    all_gather x1, blocking collectives, body(): lax.all_gather(w_kv, 'exp', axis=0, tiled=True)  137 us
    all_gather x1, waiting for transfers between devices, body(): gathered = lax.all_gather(received, 'ctx', axis=0, tiled=True)  79.6 us
    all_gather x1, waiting for transfers between devices, body(): lax.all_gather(w_query, 'exp', axis=0, tiled=True)  79.1 us
    reduce_scatter x1, waiting for transfers between devices, body(): lax.psum_scatter(jnp.einsum('ref,efd->red', hidden, w_down, preferred_ele...  49.2 us
    all_gather x1, blocking collectives, body(): value_piece = lax.all_gather(values, 'ctx', axis=0, tiled=True)  33.4 us
    all_to_all x1, blocking collectives, body(): lax.all_to_all(buffer.reshape(capacity, experts, features), 'exp', split_...  24.6 us
    all_to_all x1, waiting for transfers between devices, body(): lax.all_to_all(summed, 'exp', split_axis=0, concat_axis=1, tiled=True)  20.5 us
  transfers between devices with their start and end apart: 5, of which 5 were waited for; matrix products, arithmetic and copies ran while one was open for 2% of the time, Pallas kernels for 0%

commit v1 on v0

--- a/solution.py
+++ b/solution.py
@@ -1,10 +1,16 @@
+import functools
+
 import jax
 import jax.numpy as jnp
 from jax import lax
+from jax.experimental import pallas as pl
+from jax.experimental.pallas import tpu as pltpu
 from jax.sharding import PartitionSpec as P
 
 HD = 128
 TOP = 2
+MESH = pl.DeviceIdType.MESH
+NX, NY, NZ = 4, 4, 8
 
 
 epsilon = 1e-06
@@ -12,6 +18,131 @@
 
 def rms_scaled(values):
     return values * lax.rsqrt(jnp.mean(values * values, axis=-1, keepdims=True) + epsilon)
+
+
+def here():
+    ctx, exp = lax.axis_index("ctx"), lax.axis_index("exp")
+    core, y = ctx % 2, exp % NY
+    z, x_lo = (exp // NY) % NZ, exp // (NY * NZ)
+    return (ctx // 2) * 2 + x_lo, y, z, core
+
+
+def device(x, y, z, core):
+    return (x // 2) * 2 + core, ((x % 2) * NZ + z) * NY + y
+
+
+def signal(sem, target):
+    pl.semaphore_signal(sem, inc=1, device_id=target, device_id_type=MESH)
+
+
+CHUNKS = ((0, 0, 256), (0, 256, 256), (1, 0, 128), (2, 0, 256), (2, 256, 256))
+
+
+def gather_kernel(q_in, kv_in, o_in, q_out, kv_out, o_out, own_sem, z_send, z_recv, y_send, y_recv, x_send, x_recv, s_send, s_recv):
+    x, y, z, core = here()
+    x_lo = x % 2
+    ins, outs = (q_in, kv_in, o_in), (q_out, kv_out, o_out)
+    barrier = pltpu.get_barrier_semaphore()
+    partners = [device(x, y, (z + k) % NZ, core) for k in range(1, NZ)]
+    partners += [device(x, (y + k) % NY, z, core) for k in range(1, NY)]
+    partners += [device((x + k) % NX, y, z, core) for k in (1, 3)]
+    partners += [device(x, y, z, 1 - core)]
+    for partner in partners:
+        signal(barrier, partner)
+
+    def cols(chunk):
+        array, first, width = CHUNKS[chunk]
+        half = ins[array].shape[1] // 2
+        return array, pl.ds(pl.multiple_of(core * half + first, 128), width)
+
+    own = []
+    for chunk in range(len(CHUNKS)):
+        array, where = cols(chunk)
+        copy = pltpu.make_async_copy(ins[array].at[:, where], outs[array].at[x_lo, z, y, :, where], own_sem.at[chunk])
+        copy.start()
+        own.append(copy)
+    pl.semaphore_wait(barrier, len(partners))
+
+    def remote(src, dst, send, recv, target):
+        return pltpu.make_async_remote_copy(src_ref=src, dst_ref=dst, send_sem=send, recv_sem=recv, device_id=target, device_id_type=MESH)
+
+    for chunk in range(len(CHUNKS)):
+        array, where = cols(chunk)
+        for k in (4, 3, 5, 2, 6, 1, 7):
+            remote(ins[array].at[:, where], outs[array].at[x_lo, z, y, :, where], z_send.at[chunk], z_recv.at[chunk],
+                   device(x, y, (z + k) % NZ, core)).start()
+
+    def z_wait(chunk):
+        array, where = cols(chunk)
+        seven = outs[array].at[x_lo, pl.ds(0, NZ - 1), y, :, where]
+        return remote(seven, seven, z_send.at[chunk], z_recv.at[chunk], partners[0])
+
+    def y_step(chunk):
+        array, where = cols(chunk)
+        z_wait(chunk).wait_recv()
+        own[chunk].wait()
+        block = outs[array].at[x_lo, :, y, :, where]
+        for k in (2, 1, 3):
+            remote(block, block, y_send.at[chunk], y_recv.at[chunk], device(x, (y + k) % NY, z, core)).start()
+
+    def y_wait(chunk):
+        array, where = cols(chunk)
+        three = outs[array].at[x_lo, :, pl.ds(0, NY - 1), :, where]
+        return remote(three, three, y_send.at[chunk], y_recv.at[chunk], partners[0])
+
+    def x_step(chunk):
+        array, where = cols(chunk)
+        y_wait(chunk).wait_recv()
+        for k, first in ((1, 0), (3, NZ // 2)):
+            part = outs[array].at[x_lo, pl.ds(first, NZ // 2), :, :, where]
+            remote(part, part, x_send.at[chunk], x_recv.at[chunk], device((x + k) % NX, y, z, core)).start()
+        part = outs[array].at[x_lo, :, :, :, where]
+        remote(part, part, s_send.at[chunk], s_recv.at[chunk], device(x, y, z, 1 - core)).start()
+
+    def x_wait(chunk):
+        array, where = cols(chunk)
+        mine, other = outs[array].at[x_lo, :, :, :, where], outs[array].at[1 - x_lo, :, :, :, where]
+        return remote(mine, other, x_send.at[chunk], x_recv.at[chunk], partners[0])
+
+    def s_step(chunk):
+        array, where = cols(chunk)
+        x_wait(chunk).wait_recv()
+        part = outs[array].at[1 - x_lo, :, :, :, where]
+        remote(part, part, s_send.at[chunk], s_recv.at[chunk], device(x, y, z, 1 - core)).start()
+
+    n = len(CHUNKS)
+    for step in range(n + 2):
+        if step < n:
+            y_step(step)
+        if 0 <= step - 1 < n:
+            x_step(step - 1)
+        if 0 <= step - 2 < n:
+            s_step(step - 2)
+    for chunk in range(n):
+        array, first, width = CHUNKS[chunk]
+        half = ins[array].shape[1] // 2
+        theirs = pl.ds(pl.multiple_of((1 - core) * half + first, 128), width)
+        _, where = cols(chunk)
+        both = remote(outs[array].at[:, :, :, :, where], outs[array].at[:, :, :, :, theirs], s_send.at[chunk], s_recv.at[chunk], partners[0])
+        both.wait_recv()
+        both.wait_send()
+        z_wait(chunk).wait_send()
+        y_wait(chunk).wait_send()
+        x_wait(chunk).wait_send()
+
+
+def gather_weights(*weights):
+    n = len(CHUNKS)
+    outs = pl.pallas_call(
+        gather_kernel,
+        out_shape=[jax.ShapeDtypeStruct((2, NZ, NY) + w.shape, w.dtype) for w in weights],
+        in_specs=[pl.BlockSpec(memory_space=pl.ANY)] * 3,
+        out_specs=[pl.BlockSpec(memory_space=pl.ANY)] * 3,
+        scratch_shapes=[pltpu.SemaphoreType.DMA((n,))] * 9,
+        compiler_params=pltpu.CompilerParams(collective_id=0, has_side_effects=True),
+        name="gather_weights",
+    )(*weights)
+    return [o.reshape(-1, o.shape[-1]) for o in outs]
 
 
 def body(
@@ -20,11 +151,7 @@
     features = tokens.shape[-1]
     inputs = tokens.reshape(-1, features)
     tok_rows = inputs.shape[0]
-    full_query, full_kv, full_out = (
-        lax.all_gather(w_query, "exp", axis=0, tiled=True),
-        lax.all_gather(w_kv, "exp", axis=0, tiled=True),
-        lax.all_gather(w_out, "exp", axis=0, tiled=True),
-    )
+    full_query, full_kv, full_out = gather_weights(w_query, w_kv, w_out)
     floats = inputs.astype(jnp.float32)
     attn_in = (rms_scaled(floats) * attn_gain).astype(jnp.bfloat16)
     head_count = full_query.shape[1] // HD

time: 809 us -> 280 us (0.35)
  waiting for transfers between devices: 519 us -> 104 us
  blocking collectives: 202 us -> 48.5 us
  Pallas kernels: 0 us -> 39.2 us
    all_gather x2 -> x0, waiting for transfers between devices: 368 us -> none  [the longest x1 289 us: body(): lax.all_gather(w_out, 'exp', axis=0, tiled=True)]
    all_gather x1 -> x0, blocking collectives: 137 us -> none  [body(): lax.all_gather(w_kv, 'exp', axis=0, tiled=True)]
    all_gather x1, waiting for transfers between devices: 79.6 us -> 34.3 us  [body(): gathered = lax.all_gather(received, 'ctx', axis=0, tiled=True)]
    pallas_call x0 -> x1, Pallas kernels: none -> 39.2 us  [gather_weights(): pl.pallas_call(gather_kernel, out_shape=[jax.ShapeDtypeStruct((2, NZ, NY)...]
    all_gather x1, blocking collectives: 33.4 us -> 6.92 us  [body(): value_piece = lax.all_gather(values, 'ctx', axis=0, tiled=True)]
    all_to_all x1, blocking collectives: 24.6 us -> 34.7 us  [body(): lax.all_to_all(buffer.reshape(capacity, experts, features), 'exp', split_...]
  transfers between devices with their start and end apart: 5 -> 3, of which waited for: 5 -> 3; matrix products, arithmetic and copies ran while one was open for 2% -> 0% of each run, Pallas kernels for 0% -> 0%
where the time goes in v1:
time: 280 us; the launch traced here: 278 us
  waiting for transfers between devices  104 us (37%)
  blocking collectives  48.5 us (17%)
  Pallas kernels  39.2 us (14%)
  matrix products  26.2 us (9%)
  local copies, waits for them, and re-layouts  22.2 us (8%)
  between operations  14.3 us (5%)
  other arithmetic  12.7 us (5%)
  starting transfers between devices  10.7 us (4%)
    reduce_scatter x1, waiting for transfers between devices, body(): lax.psum_scatter(jnp.einsum('ref,efd->red', hidden, w_down, preferred_ele...  49.2 us
    pallas_call x1, Pallas kernels, gather_weights(): pl.pallas_call(gather_kernel, out_shape=[jax.ShapeDtypeStruct((2, NZ, NY)...  39.2 us
    all_to_all x1, blocking collectives, body(): lax.all_to_all(buffer.reshape(capacity, experts, features), 'exp', split_...  34.7 us
    all_gather x1, waiting for transfers between devices, body(): gathered = lax.all_gather(received, 'ctx', axis=0, tiled=True)  34.3 us
    all_to_all x1, waiting for transfers between devices, body(): lax.all_to_all(summed, 'exp', split_axis=0, concat_axis=1, tiled=True)  20.5 us
    dot_general x1, matrix products, body(): jnp.einsum('ref,efd->red', hidden, w_down, preferred_element_type=jnp.flo...  11.7 us
    all_to_all x1, starting transfers between devices, body(): lax.all_to_all(summed, 'exp', split_axis=0, concat_axis=1, tiled=True)  10.4 us
    dot_general x1, matrix products, body(): jnp.einsum('red,edf->ref', gathered, w_gate, preferred_element_type=jnp.f...  7.25 us
  transfers between devices with their start and end apart: 3, of which 3 were waited for; matrix products, arithmetic and copies ran while one was open for 0% of the time, Pallas kernels for 0%

profile of v1, /device:TPU:1, one launch (start us, length us, event | category | flops | bytes accessed | tf_op | source)
XLA Modules:
  0.0 277.9 jit_solution(14027266186943430544)
XLA Ops:
  7.2 0.9 copy.51
  8.2 0.1 reshape_reshape.3
  8.3 0.1 eq.42
  8.4 0.1 eq.38
  8.6 1.1 fusion.18
  9.7 39.2 %gather_weights.1 = (bf16[2,8,4,16,1024]{4,3,2,1,0:T(8,128)(2,1)}, bf16[2,8,4,16,256]{4,3,2,1,0:T(8,128)(2,1)}, bf16[2,8,4,16,1024]{4,3,2,1,0:T(8,128)(2,1)}) custom-call(bf16[16,1024]{1,0:T(8,128)(2,1)} %q_in.1, bf16[16,256]{1,0:T(8,128)(2,1)} %kv_in.1, bf16[16,1024]{1,0:T(8,128)(2,1)} %o_in.1), custom_call_target="tpu_custom_call" | custom-call | tf_op jit(solution)/shard_map/gather_weights/pallas_call | solution.py:136
  48.9 1.4 fusion.26
  50.3 0.1 multiply_reduce_fusion.3
  50.5 0.6 reduce-window.6
  51.1 0.2 slice_reduce_fusion
  51.3 0.1 fusion.33
  51.5 4.0 %copy.48 = bf16[1024,1024]{1,0:T(8,128)(2,1)} copy(bf16[1024,1024]{0,1:T(8,128)(2,1)} %bitcast.141) | data formatting | bytes 4194304 | tf_op jit(solution)/shard_map/dot_general | solution.py:158
  55.5 2.5 multiply_reduce_fusion.2
  58.0 0.1 multiply_convert_fusion.2
  58.1 6.9 %all_gather.10 = bf16[512,128]{1,0:T(8,128)(2,1)S(1)} all-gather(bf16[128,128]{1,0:T(8,128)(2,1)S(1)} %slice.36), channel_id=1, replica_groups=mesh['ctx'=4,'exp'=64] {'ctx'}, dimensions={0}, use_global_device_ids=true | all-gather | bytes 163840 | tf_op jit(solution)/shard_map/all_gather | solution.py:167
  65.0 6.9 %all_gather.9 = bf16[512,128]{1,0:T(8,128)(2,1)S(1)} all-gather(bf16[128,128]{1,0:T(8,128)(2,1)S(1)} %multiply_convert_fusion.2), channel_id=1, replica_groups=mesh['ctx'=4,'exp'=64] {'ctx'}, dimensions={0}, use_global_device_ids=true | all-gather | bytes 163840 | tf_op jit(solution)/shard_map/all_gather | solution.py:166
  72.0 0.2 multiply_convert_fusion.1
  72.2 0.5 convert_reduce_fusion
  72.7 0.5 fusion.15
  73.2 0.1 reshape.182
  73.4 2.1 multiply_reduce_fusion.1
  75.5 0.7 copy-done.2
  76.2 0.1 multiply_convert_fusion
  76.3 0.3 broadcast_in_dim.19
  76.6 1.0 reshape.208
  77.6 2.4 scatter_custom_fusion
  80.0 0.4 copy.55
  80.5 34.7 %all_to_all.33 = bf16[6,64,1024]{2,0,1:T(8,128)(2,1)S(1)} all-to-all(bf16[6,64,1024]{2,0,1:T(8,128)(2,1)S(1)} %copy.55), channel_id=1, replica_groups=mesh['ctx'=4,'exp'=64] {'exp'}, dimensions={1} | all-to-all | bytes 1572864 | tf_op jit(solution)/shard_map/all_to_all | solution.py:201
  115.1 1.1 all_to_all.27
  116.3 0.2 reduce-scatter.2.cloned.1.call-start
  116.5 34.3 %all-gather.2.cloned.1.call-done = bf16[1536,1,1024]{2,0,1:T(8,128)(2,1)} async-done(((bf16[384,1,1024]{2,0,1:T(8,128)(2,1)}), bf16[1536,1,1024]{2,0,1:T(8,128)(2,1)}) %all-gather.2.cloned.1.call-update) | async-done | bytes 3145744 | tf_op jit(solution)/shard_map/all_gather | solution.py:204
  150.8 7.3 %fusion.7 = f32[1536,1024]{1,0:T(8,128)} fusion(bf16[1536,1,1024]{2,0,1:T(8,128)(2,1)} %all-gather.2.cloned.1.call-done, bf16[1,1024,1024]{2,1,0:T(8,128)(2,1)S(1)} %copy-done), kind=kOutput, calls=%fused_computation.13 | convolution fusion | flops 3221225472 | bytes 11534336 | tf_op jit(solution)/shard_map/red,edf->ref/dot_general | solution.py:205
  158.1 11.7 %fusion.4 = bf16[1536,1,1024]{2,0,1:T(8,128)(2,1)} fusion(f32[1536,1024]{1,0:T(8,128)} %fusion.7, bf16[1536,1,1024]{2,0,1:T(8,128)(2,1)} %all-gather.2.cloned.1.call-done, bf16[1,1024,1024]{2,1,0:T(8,128)(2,1)} %param.21, bf16[1,1024,1024]{2,1,0:T(8,128)(2,1)} %param.20), kind=kOutput, calls=%fused_computation.10 | convolution fusion | flops 6453460992 | bytes 16777216 | tf_op jit(solution)/shard_map/ref,efd->red/dot_general | solution.py:209
  169.8 49.2 %reduce-scatter.2.cloned.1.call-done = bf16[384,1,1024]{2,0,1:T(8,128)(2,1)} async-done(((bf16[1536,1,1024]{2,0,1:T(8,128)(2,1)}), bf16[384,1,1024]{2,0,1:T(8,128)(2,1)}) %reduce-scatter.2.cloned.1.call-update) | async-done | bytes 786448 | tf_op jit(solution)/shard_map/reduce_scatter | solution.py:208
  219.0 0.5 broadcast.147
  219.5 2.4 reduce.3
  221.9 1.4 reshape.217
  223.3 10.4 %all-to-all-start.1 = ((bf16[64,2,3072]{2,1,0:T(2,128)(2,1)}), bf16[64,2,3072]{2,1,0:T(2,128)(2,1)S(1)}, u32[]{:S(2)}, u32[]{:S(2)}) async-start(bf16[64,2,3072]{2,1,0:T(2,128)(2,1)} %reshape.217), calls=%async_computation.2 | async-start | bytes 1572864 | tf_op jit(solution)/shard_map/all_to_all | solution.py:216
  233.7 0.2 fusion.36
  234.0 0.1 copy.50
  234.1 20.5 %all-to-all-done.1 = bf16[64,2,3072]{2,1,0:T(2,128)(2,1)S(1)} async-done(((bf16[64,2,3072]{2,1,0:T(2,128)(2,1)}), bf16[64,2,3072]{2,1,0:T(2,128)(2,1)S(1)}, u32[]{:S(2)}, u32[]{:S(2)}) %all-to-all-start.1) | async-done | bytes 786464 | tf_op jit(solution)/shard_map/all_to_all | solution.py:216
  254.7 2.0 reshape.218
  256.6 5.8 %reduce.1 = bf16[384,1024]{1,0:T(8,128)(2,1)S(1)} reduce(bf16[384,1,1024]{2,1,0:T(2,128)(2,1)} %reshape.218, bf16[]{:T(256)} %constant.42), dimensions={1}, to_apply=%all_to_all.28.reduce_sub_computation | reduce | bytes 1572866 | tf_op jit(solution)/shard_map/all_to_all | solution.py:216
  262.4 1.2 all_to_all.29
  263.6 1.7 copy.57
  265.3 2.0 gather_fusion
  267.3 1.7 reshape.195
  269.0 2.1 multiply_reduce_fusion
  (30 shorter events, 0.3 us)
Async XLA Ops:
  7.2 143.7 %copy-start = (bf16[1,1024,1024]{2,1,0:T(8,128)(2,1)S(1)}, bf16[1,1024,1024]{2,1,0:T(8,128)(2,1)}, u32[]{:S(2)}) copy-start(bf16[1,1024,1024]{2,1,0:T(8,128)(2,1)} %param.19) | copy-start | bytes 6291460
  7.2 143.7 %all-gather.2.cloned.1.call-start = ((), (), s32[]{:S(2)}) async-start(), calls=%async_computation.3 | async-start | bytes 3932160 | tf_op jit(solution)/shard_map/all_gather | solution.py:204
  51.4 4.0 %copy-start.1 = (bf16[1,128,1024]{2,1,0:T(8,128)(2,1)S(1)}, bf16[1,128,1024]{2,1,0:T(8,128)(2,1)}, u32[]{:S(2)}) copy-start(bf16[1,128,1024]{2,1,0:T(8,128)(2,1)} %param.11) | copy-start | bytes 786436
  51.5 4.0 %copy-start.4 = (f32[1024]{0:T(1024)S(1)}, f32[1024]{0:T(1024)}, u32[]{:S(2)}) copy-start(f32[1024]{0:T(1024)} %param.13) | copy-start | bytes 12292
  73.2 3.0 %copy-start.5 = (f32[1024]{0:T(1024)S(1)}, f32[1024]{0:T(1024)}, u32[]{:S(2)}) copy-start(f32[1024]{0:T(1024)} %param.17) | copy-start | bytes 12292
  75.5 0.7 copy-start.2
  116.3 102.7 %reduce-scatter.2.cloned.1.call-start = ((), (), s32[]{:S(2)}) async-start(), calls=%async_computation.4 | async-start | bytes 3932160 | tf_op jit(solution)/shard_map/reduce_scatter | solution.py:208
  219.5 14.2 %copy-start.3 = (bf16[1024,64]{0,1:T(8,128)(2,1)S(1)}, bf16[1024,64]{0,1:T(8,128)(2,1)}, u32[]{:S(2)}) copy-start(bf16[1024,64]{0,1:T(8,128)(2,1)} %param.18) | copy-start | bytes 393220
  221.9 12.0 %copy-start.6 = (s32[1,128,2]{1,2,0:T(2,128)S(1)}, s32[1,128,2]{1,2,0:T(2,128)}, u32[]{:S(2)}) copy-start(s32[1,128,2]{1,2,0:T(2,128)} %param.12) | copy-start | bytes 3076
  223.3 31.4 %all-to-all-start.1 = ((bf16[64,2,3072]{2,1,0:T(2,128)(2,1)}), bf16[64,2,3072]{2,1,0:T(2,128)(2,1)S(1)}, u32[]{:S(2)}, u32[]{:S(2)}) async-start(bf16[64,2,3072]{2,1,0:T(2,128)(2,1)} %reshape.217), calls=%async_computation.2 | async-start | bytes 1572864 | tf_op jit(solution)/shard_map/all_to_all | solution.py:216
Sparse Core Ops, SparseCore 0:
  116.4 34.3 all-gather.1
  169.9 49.0 reduce-scatter.1

commit v2 on v1

--- a/solution.py
+++ b/solution.py
@@ -143,6 +143,207 @@
         name="gather_weights",
     )(*weights)
     return [o.reshape(-1, o.shape[-1]) for o in outs]
+
+
+CAP = 6
+DRAIN = 256
+
+
+def expert_kernel(pos_ref, pair_ref, gate_ref, moe_ref, wg_hbm, wu_hbm, wd_hbm, out_ref,
+                  wg, wu, wd, sent, came, rows, hidden, terms, theirs, halves, sides, final, back,
+                  w_sem, zy_send, zy_recv, x_send, x_recv, s_send, s_recv, own_sem,
+                  rs_send, rs_recv, rx_send, rx_recv, rz_send, rz_recv):
+    x, y, z, core = here()
+    x_lo = x % 2
+    features = moe_ref.shape[1]
+    block = NZ * CAP
+    barrier = pltpu.get_barrier_semaphore()
+    plane = [(k, d) for d in (0, 1, 3, 2) for k in (4, 3, 5, 2, 6, 1, 7, 0) if (k, d) != (0, 0)]
+    sibling = device(x, y, z, 1 - core)
+    partners = [device(x, (y + d) % NY, (z + k) % NZ, core) for k, d in plane]
+    partners += [device((x + k) % NX, y, z, core) for k in range(1, NX)] + [sibling]
+    for partner in partners:
+        signal(barrier, partner)
+    loads = [pltpu.make_async_copy(src.at[0], dst, w_sem.at[i]) for i, (src, dst) in enumerate(((wg_hbm, wg), (wu_hbm, wu), (wd_hbm, wd)))]
+    for load in loads:
+        load.start()
+
+    def remote(src, dst, send, recv, target):
+        return pltpu.make_async_remote_copy(src_ref=src, dst_ref=dst, send_sem=send, recv_sem=recv, device_id=target, device_id_type=MESH)
+
+    def local(src, dst, sem):
+        return pltpu.make_async_copy(src, dst, sem)
+
+    row = lax.broadcasted_iota(jnp.int32, (2 * NZ * NY * CAP, pos_ref.shape[1]), 0)
+    chosen = jnp.where((row == pos_ref[0:1, :]) | (row == pos_ref[1:2, :]), 1.0, 0.0).astype(jnp.bfloat16)
+    sent[...] = jnp.dot(chosen, moe_ref[...], preferred_element_type=jnp.float32).astype(jnp.bfloat16).reshape(sent.shape)
+    pl.semaphore_wait(barrier, len(partners))
+
+    for k, d in plane:
+        to_z, to_y = (z + k) % NZ, (y + d) % NY
+        remote(sent.at[to_z, to_y], came.at[d, z], zy_send, zy_recv.at[d], device(x, to_y, to_z, core)).start()
+    own = local(sent.at[z, y], came.at[0, z], own_sem.at[0])
+    own.start()
+
+    def zy_wait(d):
+        count = NZ if d else NZ - 1
+        return remote(came.at[d, pl.ds(0, count)], came.at[d, pl.ds(0, count)], zy_send, zy_recv.at[d], sibling)
+
+    def spread(d):
+        zy_wait(d).wait_recv()
+        if d == 0:
+            own.wait()
+        for k, part in ((2, x_lo), (1, 1 - x_lo), (3, 1 - x_lo)):
+            remote(came.at[d, :, part], rows.at[d, core, k - 1], x_send.at[d], x_recv.at[d], device((x + k) % NX, y, z, core)).start()
+        local(came.at[d, :, x_lo], rows.at[d, core, 3], own_sem.at[1 + d]).start()
+        remote(came.at[d, :, x_lo], rows.at[d, core, 3], s_send.at[d], s_recv.at[d], sibling).start()
+
+    def x_wait(d):
+        three = rows.at[d, core, pl.ds(0, 3)]
+        return remote(three, three, x_send.at[d], x_recv.at[d], sibling)
+
+    def share(d):
+        x_wait(d).wait_recv()
+        three = rows.at[d, core, pl.ds(0, 3)]
+        remote(three, three, s_send.at[d], s_recv.at[d], sibling).start()
+
+    def s_wait(d):
+        return remote(rows.at[d, core], rows.at[d, 1 - core], s_send.at[d], s_recv.at[d], sibling)
+
+    def compute(d):
+        s_wait(d).wait_recv()
+        local(came.at[d, :, x_lo], rows.at[d, core, 3], own_sem.at[1 + d]).wait()
+        if d == 0:
+            for load in loads:
+                load.wait()
+        many = rows[d].reshape(2 * NX * block, features)
+
+        def up(tile, carry):
+            where = pl.ds(pl.multiple_of(tile * DRAIN, DRAIN), DRAIN)
+            gated = jnp.dot(many, wg[:, where], preferred_element_type=jnp.float32)
+            lifted = jnp.dot(many, wu[:, where], preferred_element_type=jnp.float32)
+            hidden[:, where] = (gated / (1.0 + jnp.exp(-gated)) * lifted).astype(jnp.bfloat16)
+            return carry
+
+        lax.fori_loop(0, wg.shape[1] // DRAIN, up, 0)
+        inner = hidden[...]
+
+        def down(tile, carry):
+            where = pl.ds(pl.multiple_of(tile * DRAIN, DRAIN), DRAIN)
+            term = jnp.dot(inner, wd[:, where], preferred_element_type=jnp.float32).astype(jnp.bfloat16)
+            terms[d, :, :, :, :, where] = term.reshape(2, NX, NZ, CAP, DRAIN)
+            return carry
+
+        lax.fori_loop(0, features // DRAIN, down, 0)
+        remote(terms.at[d, 1 - core], theirs.at[d], rs_send.at[d], rs_recv.at[d], sibling).start()
+
+    def rs_wait(d):
+        return remote(terms.at[d, 1 - core], theirs.at[d], rs_send.at[d], rs_recv.at[d], sibling)
+
+    def halve(d):
+        rs_wait(d).wait_recv()
+        halves[d] = (terms[d, core].astype(jnp.float32) + theirs[d].astype(jnp.float32)).astype(jnp.bfloat16)
+        for k in (2, 1, 3):
+            remote(halves.at[d, k - 1], sides.at[d, k - 1], rx_send.at[d], rx_recv.at[d], device((x - k + NX) % NX, y, z, core)).start()
+
+    def rx_wait(d):
+        return remote(halves.at[d, pl.ds(0, 3)], sides.at[d], rx_send.at[d], rx_recv.at[d], sibling)
+
+    def finish(d):
+        rx_wait(d).wait_recv()
+        final[d, :, x_lo] = (halves[d, 3].astype(jnp.float32) + sides[d, 1].astype(jnp.float32)).astype(jnp.bfloat16)
+        final[d, :, 1 - x_lo] = (sides[d, 0].astype(jnp.float32) + sides[d, 2].astype(jnp.float32)).astype(jnp.bfloat16)
+        for k in (4, 3, 5, 2, 6, 1, 7, 0):
+            if (k, d) == (0, 0):
+                local(final.at[d, z], back.at[y, z], own_sem.at[1 + NY]).start()
+            else:
+                to_z, to_y = (z + k) % NZ, (y - d + NY) % NY
+                remote(final.at[d, to_z], back.at[y, z], rz_send, rz_recv.at[d], device(x, to_y, to_z, core)).start()
+
+    def pick(d):
+        count, from_y = NZ if d else NZ - 1, (y + d) % NY
+        part = back.at[from_y, pl.ds(0, count)]
+        remote(part, part, rz_send, rz_recv.at[d], sibling).wait_recv()
+        if d == 0:
+            local(final.at[d, z], back.at[y, z], own_sem.at[1 + NY]).wait()
+        tokens = pair_ref.shape[0]
+        place = lax.broadcasted_iota(jnp.int32, (tokens, 2 * block), 1) + from_y * (2 * block)
+        got = back[from_y].reshape(2 * block, features)
+        total = None
+        for choice in range(TOP):
+            mine = jnp.where(place == pair_ref[:, choice:choice + 1], 1.0, 0.0).astype(jnp.bfloat16)
+            part = gate_ref[:, choice:choice + 1] * jnp.dot(mine, got, preferred_element_type=jnp.float32)
+            total = part if total is None else total + part
+        return total
+
+    spread(0)
+    spread(1)
+    share(0)
+    compute(0)
+    spread(3)
+    share(1)
+    compute(1)
+    halve(0)
+    spread(2)
+    share(3)
+    compute(3)
+    halve(1)
+    finish(0)
+    share(2)
+    compute(2)
+    halve(3)
+    finish(1)
+    halve(2)
+    finish(3)
+    finish(2)
+    total = pick(0) + pick(1)
+    total = total + pick(3)
+    total = total + pick(2)
+    out_ref[...] = total.astype(out_ref.dtype)
+
+    for d in range(NY):
+        x_wait(d).wait_send()
+        s_wait(d).wait_send()
+        rs_wait(d).wait_send()
+        rx_wait(d).wait_send()
+    for sent_ref, sem in ((came, zy_send), (final, rz_send)):
+        some = sent_ref.at[pl.ds(0, NY - 1)]
+        remote(some, some, sem, zy_recv.at[0], sibling).wait_send()
+        rest = sent_ref.at[0, pl.ds(0, NZ - 1)]
+        remote(rest, rest, sem, zy_recv.at[0], sibling).wait_send()
+
+
+def run_experts(pos, pair, gates, moe_in, w_gate, w_up, w_down):
+    tokens, features = moe_in.shape
+    width = w_gate.shape[2]
+    bf16, f32 = jnp.bfloat16, jnp.float32
+    block = (NZ, CAP, features)
+    dma, vmem = pltpu.SemaphoreType.DMA, pltpu.VMEM
+    return pl.pallas_call(
+        expert_kernel,
+        out_shape=jax.ShapeDtypeStruct((tokens, features), bf16),
+        in_specs=[pl.BlockSpec(memory_space=vmem)] * 4 + [pl.BlockSpec(memory_space=pl.ANY)] * 3,
+        out_specs=pl.BlockSpec(memory_space=vmem),
+        scratch_shapes=[
+            vmem((features, width), bf16),
+            vmem((features, width), bf16),
+            vmem((width, features), bf16),
+            vmem((NZ, NY, 2, CAP, features), bf16),
+            vmem((NY, NZ, 2, CAP, features), bf16),
+            vmem((NY, 2, NX) + block, bf16),
+            vmem((2 * NX * NZ * CAP, width), bf16),
+            vmem((NY, 2, NX) + block, bf16),
+            vmem((NY, NX) + block, bf16),
+            vmem((NY, NX) + block, bf16),
+            vmem((NY, NX - 1) + block, bf16),
+            vmem((NY, NZ, 2, CAP, features), bf16),
+            vmem((NY, NZ, 2, CAP, features), bf16),
+            dma((3,)), dma, dma((NY,)), dma((NY,)), dma((NY,)), dma((NY,)), dma((NY,)), dma((2 + NY,)),
+            dma((NY,)), dma((NY,)), dma((NY,)), dma((NY,)), dma, dma((NY,)),
+        ],
+        compiler_params=pltpu.CompilerParams(collective_id=1, has_side_effects=True, vmem_limit_bytes=60 << 20),
+        name="run_experts",
+    )(pos, pair, gates, moe_in, w_gate, w_up, w_down)
 
 
 def body(
@@ -190,36 +391,11 @@
     gates = jnp.stack([first, 1.0 - first], axis=1)
     counts = match.reshape(tok_rows * TOP, experts).astype(jnp.int32)
     earlier = jnp.cumsum(counts, axis=0) - counts
-    slot = jnp.sum(earlier * counts, axis=1)
-    capacity = max(2, 3 * tok_rows * TOP // (2 * experts))
-    position = slot * experts + pair_ids.reshape(-1)
-    buffer = (
-        jnp.zeros((capacity * experts, features), jnp.bfloat16)
-        .at[position]
-        .set(jnp.repeat(moe_in, TOP, axis=0))
-    )
-    received = lax.all_to_all(
-        buffer.reshape(capacity, experts, features), "exp", split_axis=1, concat_axis=0, tiled=True
-    )
-    gathered = lax.all_gather(received, "ctx", axis=0, tiled=True)
-    gated = jnp.einsum("red,edf->ref", gathered, w_gate, preferred_element_type=jnp.float32)
-    lifted = jnp.einsum("red,edf->ref", gathered, w_up, preferred_element_type=jnp.float32)
-    hidden = (jax.nn.silu(gated) * lifted).astype(jnp.bfloat16)
-    summed = lax.psum_scatter(
-        jnp.einsum("ref,efd->red", hidden, w_down, preferred_element_type=jnp.float32).astype(
-            jnp.bfloat16
-        ),
-        "ctx",
-        scatter_dimension=0,
-        tiled=True,
-    )
-    returned = lax.all_to_all(summed, "exp", split_axis=0, concat_axis=1, tiled=True)
-    picked = returned.reshape(capacity * experts, features)[position].reshape(
-        tok_rows, TOP, features
-    )
-    expert_mix = jnp.sum(gates[:, :, None] * picked.astype(jnp.float32), axis=1).astype(
-        jnp.bfloat16
-    )
+    slot = jnp.sum(earlier * counts, axis=1).reshape(tok_rows, TOP)
+    chip = pair_ids % (NZ * NY)
+    sent_place = (chip * 2 + pair_ids // (NZ * NY)) * CAP + slot
+    back_place = (((chip % NY) * NZ + chip // NY) * 2 + pair_ids // (NZ * NY)) * CAP + slot
+    expert_mix = run_experts(sent_place.T, back_place, gates, moe_in, w_gate, w_up, w_down)
     return (attention_out.reshape(tokens.shape), expert_mix.reshape(tokens.shape))
 
 

time: 280 us -> 150 us (0.54)
  waiting for transfers between devices: 104 us -> 0 us
  Pallas kernels: 39.2 us -> 120 us
  blocking collectives: 48.5 us -> 14.2 us
  matrix products: 26.2 us -> 4.15 us
  local copies, waits for them, and re-layouts: 22.2 us -> 6.92 us
  between operations: 14.3 us -> 0.89 us
  starting transfers between devices: 10.7 us -> 0 us
  other arithmetic: 12.7 us -> 3.21 us
    pallas_call x0 -> x1, Pallas kernels: none -> 80.7 us  [run_experts(): pl.pallas_call(expert_kernel, out_shape=jax.ShapeDtypeStruct((tokens, fea...]
    reduce_scatter x1 -> x0, waiting for transfers between devices: 49.2 us -> none  [body(): lax.psum_scatter(jnp.einsum('ref,efd->red', hidden, w_down, preferred_ele...]
    all_to_all x1 -> x0, blocking collectives: 34.7 us -> none  [body(): lax.all_to_all(buffer.reshape(capacity, experts, features), 'exp', split_...]
    all_gather x1 -> x0, waiting for transfers between devices: 34.3 us -> none  [body(): gathered = lax.all_gather(received, 'ctx', axis=0, tiled=True)]
    all_to_all x1 -> x0, waiting for transfers between devices: 20.5 us -> none  [body(): lax.all_to_all(summed, 'exp', split_axis=0, concat_axis=1, tiled=True)]
    dot_general x2 -> x0, matrix products: 18.9 us -> none  [the longest x1 11.7 us: body(): jnp.einsum('ref,efd->red', hidden, w_down, preferred_element_type=jnp.flo...]
    all_to_all x1 -> x0, starting transfers between devices: 10.4 us -> none  [body(): lax.all_to_all(summed, 'exp', split_axis=0, concat_axis=1, tiled=True)]
    all_to_all x1 -> x0, other arithmetic: 5.76 us -> none  [body(): lax.all_to_all(summed, 'exp', split_axis=0, concat_axis=1, tiled=True)]
  transfers between devices with their start and end apart: 3 -> 0, of which waited for: 3 -> 0; matrix products, arithmetic and copies ran while one was open for 0% -> 0% of each run, Pallas kernels for 0% -> 0%
where the time goes in v2:
time: 150 us; the launch traced here: 149 us
  Pallas kernels  120 us (80%)
  blocking collectives  14.2 us (9%)
  local copies, waits for them, and re-layouts  6.92 us (5%)
  matrix products  4.15 us (3%)
  other arithmetic  3.21 us (2%)
    pallas_call x1, Pallas kernels, run_experts(): pl.pallas_call(expert_kernel, out_shape=jax.ShapeDtypeStruct((tokens, fea...  80.7 us
    pallas_call x1, Pallas kernels, gather_weights(): pl.pallas_call(gather_kernel, out_shape=[jax.ShapeDtypeStruct((2, NZ, NY)...  39.2 us
    all_gather x1, blocking collectives, body(): value_piece = lax.all_gather(values, 'ctx', axis=0, tiled=True)  7.25 us
    all_gather x1, blocking collectives, body(): key_piece = lax.all_gather(keys, 'ctx', axis=0, tiled=True)  6.92 us

profile of v2, /device:TPU:1, one launch (start us, length us, event | category | flops | bytes accessed | tf_op | source)
XLA Modules:
  0.0 149.3 jit_solution(4750585055386992848)
XLA Ops:
  0.6 0.0 copy-start
  0.6 39.2 %gather_weights.1 = (bf16[2,8,4,16,1024]{4,3,2,1,0:T(8,128)(2,1)}, bf16[2,8,4,16,256]{4,3,2,1,0:T(8,128)(2,1)}, bf16[2,8,4,16,1024]{4,3,2,1,0:T(8,128)(2,1)}) custom-call(bf16[16,1024]{1,0:T(8,128)(2,1)} %q_in.1, bf16[16,256]{1,0:T(8,128)(2,1)} %kv_in.1, bf16[16,1024]{1,0:T(8,128)(2,1)} %o_in.1), custom_call_target="tpu_custom_call" | custom-call | tf_op jit(solution)/shard_map/gather_weights/pallas_call | solution.py:136
  39.9 1.1 fusion.3
  41.0 1.4 fusion.9
  42.4 0.1 multiply_reduce_fusion.2
  42.5 0.1 multiply_convert_fusion.2
  42.6 6.9 %all_gather.6 = bf16[512,128]{1,0:T(8,128)(2,1)S(1)} all-gather(bf16[128,128]{1,0:T(8,128)(2,1)S(1)} %multiply_convert_fusion.2), channel_id=1, replica_groups=mesh['ctx'=4,'exp'=64] {'ctx'}, dimensions={0}, use_global_device_ids=true | all-gather | bytes 163840 | tf_op jit(solution)/shard_map/all_gather | solution.py:367
  49.6 0.0 copy-start.1
  49.6 0.0 copy-start.5
  49.6 2.9 %copy.34 = bf16[1024,1024]{1,0:T(8,128)(2,1)S(1)} copy(bf16[1024,1024]{0,1:T(8,128)(2,1)} %bitcast.76) | data formatting | bytes 4194304 | tf_op jit(solution)/shard_map/dot_general | solution.py:359
  52.5 0.0 copy-done.1
  52.5 0.0 copy-done.5
  52.5 0.9 multiply_reduce_fusion.1
  53.4 0.2 multiply_convert_fusion.1
  53.7 0.5 convert_reduce_fusion
  54.2 0.0 copy-start.3
  54.2 7.2 %all_gather.7 = bf16[512,128]{1,0:T(8,128)(2,1)S(1)} all-gather(bf16[128,128]{1,0:T(8,128)(2,1)S(1)} %slice.34), channel_id=1, replica_groups=mesh['ctx'=4,'exp'=64] {'ctx'}, dimensions={0}, use_global_device_ids=true | all-gather | bytes 163840 | tf_op jit(solution)/shard_map/all_gather | solution.py:368
  61.5 0.5 fusion
  62.0 0.0 copy-start.6
  62.0 0.1 reshape.120
  62.1 0.0 copy-start.7
  62.1 0.0 copy-done.3
  62.1 0.5 multiply_reduce_fusion
  62.7 0.0 copy-start.4
  62.7 0.0 copy-done.6
  62.7 0.1 multiply_convert_fusion.moe_ref
  62.8 0.0 copy-done
  62.8 0.0 copy-start.2
  62.9 0.2 fusion.30
  63.1 0.0 copy-done.7
  63.1 0.1 copy.36
  63.2 0.1 copy.40
  63.3 0.8 copy.42.gate_ref
  64.1 0.1 eq.39
  64.2 0.6 reduce-window.6
  64.8 0.2 slice_reduce_fusion
  65.1 0.1 eq.35
  65.2 0.1 fusion.22
  65.3 0.1 reshape.125
  65.5 0.8 fusion.19
  66.2 0.6 copy.41.pos_ref
  66.9 0.0 copy-done.2
  66.9 80.7 %run_experts.1 = bf16[128,1024]{1,0:T(8,128)(2,1)} custom-call(s32[2,128]{1,0:T(2,128)} %copy.41.pos_ref, s32[128,2]{1,0:T(8,128)} %get-tuple-element.10.pair_ref, f32[128,2]{1,0:T(8,128)} %copy.42.gate_ref, bf16[128,1024]{1,0:T(8,128)(2,1)} %copy-done.2, bf16[1,1024,1024]{2,1,0:T(8,128)(2,1)} %wg_hbm.1, bf16[1,1024,1024]{2,1,0:T(8,128)(2,1)} %wu_hbm.1, ...), custom_call_target="tpu_custom_call" | custom-call | tf_op jit(solution)/shard_map/run_experts/pallas_call | solution.py:322
  147.6 0.0 copy-done.4
  147.6 1.7 %copy.52 = bf16[1,128,1024]{2,1,0:T(8,128)(2,1)} copy(bf16[1,128,1024]{2,1,0:T(8,128)(2,1)} %bitcast.78) | data formatting | bytes 524288
  (11 shorter events, 0.2 us)
Async XLA Ops:
  0.6 62.2 %copy-start = (bf16[1024,64]{0,1:T(8,128)(2,1)S(1)}, bf16[1024,64]{0,1:T(8,128)(2,1)}, u32[]{:S(2)}) copy-start(bf16[1024,64]{0,1:T(8,128)(2,1)} %param.18) | copy-start | bytes 393220
  49.6 2.9 %copy-start.1 = (bf16[1,128,1024]{2,1,0:T(8,128)(2,1)S(1)}, bf16[1,128,1024]{2,1,0:T(8,128)(2,1)}, u32[]{:S(2)}) copy-start(bf16[1,128,1024]{2,1,0:T(8,128)(2,1)} %param.11) | copy-start | bytes 786436
  49.6 2.9 %copy-start.5 = (f32[1024]{0:T(1024)S(1)}, f32[1024]{0:T(1024)}, u32[]{:S(2)}) copy-start(f32[1024]{0:T(1024)} %param.13) | copy-start | bytes 12292
  54.2 7.9 %copy-start.3 = (bf16[2,8,4,16,1024]{4,3,2,1,0:T(8,128)(2,1)S(1)}, bf16[2,8,4,16,1024]{4,3,2,1,0:T(8,128)(2,1)}, u32[]{:S(2)}) copy-start(bf16[2,8,4,16,1024]{4,3,2,1,0:T(8,128)(2,1)} %get-tuple-element.7) | copy-start | bytes 6291460
  62.0 0.7 copy-start.6
  62.1 1.0 copy-start.7
  62.7 84.9 %copy-start.4 = (bf16[128,1024]{1,0:T(8,128)(2,1)}, bf16[128,1024]{1,0:T(8,128)(2,1)S(1)}, u32[]{:S(2)}) copy-start(bf16[128,1024]{1,0:T(8,128)(2,1)S(1)} %get-tuple-element.17) | copy-start | bytes 786436
  62.8 4.0 %copy-start.2 = (bf16[128,1024]{1,0:T(8,128)(2,1)}, bf16[128,1024]{1,0:T(8,128)(2,1)S(1)}, u32[]{:S(2)}) copy-start(bf16[128,1024]{1,0:T(8,128)(2,1)S(1)} %multiply_convert_fusion.moe_ref) | copy-start | bytes 786436

commit v3 on v2

v3 whole, which is shorter than its diff:
```python
import functools

import jax
import jax.numpy as jnp
from jax import lax
from jax.experimental import pallas as pl
from jax.experimental.pallas import tpu as pltpu
from jax.sharding import PartitionSpec as P

HD = 128
TOP = 2
MESH = pl.DeviceIdType.MESH
NX, NY, NZ = 4, 4, 8


epsilon = 1e-06
bf16, f32 = jnp.bfloat16, jnp.float32


def rms_scaled(values):
    return values * lax.rsqrt(jnp.mean(values * values, axis=-1, keepdims=True) + epsilon)


def here():
    ctx, exp = lax.axis_index("ctx"), lax.axis_index("exp")
    core, y = ctx % 2, exp % NY
    z, x_lo = (exp // NY) % NZ, exp // (NY * NZ)
    return (ctx // 2) * 2 + x_lo, y, z, core


def device(x, y, z, core):
    return (x // 2) * 2 + core, ((x % 2) * NZ + z) * NY + y


def signal(sem, target):
    pl.semaphore_signal(sem, inc=1, device_id=target, device_id_type=MESH)


CHUNKS = ((1, 0, 128), (0, 0, 256), (0, 256, 256), (2, 0, 256), (2, 256, 256))
TILE = 256
CAP = 6
DRAIN = 256


def remote(src, dst, send, recv, target):
    return pltpu.make_async_remote_copy(src_ref=src, dst_ref=dst, send_sem=send, recv_sem=recv, device_id=target, device_id_type=MESH)


def local(src, dst, sem):
    return pltpu.make_async_copy(src, dst, sem)


def layer_kernel(tok_ref, id_ref, again_ref, mgain_ref, router_ref, q_in, kv_in, o_in, wg_hbm, wu_hbm, wd_hbm, att_ref, mix_ref,
                 q_all, kv_all, o_all, normed, queries, key_values, context, moe_ref, chosen_ref, back_ref, gate_ref,
                 wg, wu, wd, sent, came, rows, hidden, terms, theirs, halves, sides, final, back,
                 g_own, z_send, z_recv, y_send, y_recv, gx_send, gx_recv, gs_send, gs_recv, kv_send, kv_recv,
                 w_sem, zy_send, zy_recv, x_send, x_recv, s_send, s_recv, own_sem,
                 rs_send, rs_recv, rx_send, rx_recv, rz_send, rz_recv):
    x, y, z, core = here()
    x_lo = x % 2
    features = tok_ref.shape[2]
    tokens = tok_ref.shape[1]
    experts = router_ref.shape[1]
    block = NZ * CAP
    plane = [(k, d) for d in (0, 1, 3, 2) for k in (4, 3, 5, 2, 6, 1, 7, 0) if (k, d) != (0, 0)]
    sibling = device(x, y, z, 1 - core)
    barrier = pltpu.get_barrier_semaphore()
    partners = [device(x, (y + d) % NY, (z + k) % NZ, core) for k, d in plane]
    partners += [device((x + k) % NX, y, z, core) for k in range(1, NX)]
    partners += [sibling, device((x + 2) % NX, y, z, 1 - core)]
    for partner in partners:
        signal(barrier, partner)

    ins, outs = (q_in, kv_in, o_in), (q_all, kv_all, o_all)

    def cols(chunk):
        array, first, width = CHUNKS[chunk]
        half = ins[array].shape[1] // 2
        return array, pl.ds(pl.multiple_of(core * half + first, 128), width)

    own = []
    for chunk in range(len(CHUNKS)):
        array, where = cols(chunk)
        copy = local(ins[array].at[:, where], outs[array].at[x_lo, z, y, :, where], g_own.at[chunk])
        copy.start()
        own.append(copy)
    pl.semaphore_wait(barrier, len(partners))
    for chunk in range(len(CHUNKS)):
        array, where = cols(chunk)
        for k in (4, 3, 5, 2, 6, 1, 7):
            remote(ins[array].at[:, where], outs[array].at[x_lo, z, y, :, where], z_send.at[chunk], z_recv.at[chunk],
                   device(x, y, (z + k) % NZ, core)).start()

    def z_wait(chunk):
        array, where = cols(chunk)
        seven = outs[array].at[x_lo, pl.ds(0, NZ - 1), y, :, where]
        return remote(seven, seven, z_send.at[chunk], z_recv.at[chunk], sibling)

    def y_step(chunk):
        array, where = cols(chunk)
        z_wait(chunk).wait_recv()
        own[chunk].wait()
        part = outs[array].at[x_lo, :, y, :, where]
        for k in (2, 1, 3):
            remote(part, part, y_send.at[chunk], y_recv.at[chunk], device(x, (y + k) % NY, z, core)).start()

    def y_wait(chunk):
        array, where = cols(chunk)
        three = outs[array].at[x_lo, :, pl.ds(0, NY - 1), :, where]
        return remote(three, three, y_send.at[chunk], y_recv.at[chunk], sibling)

    def x_step(chunk):
        array, where = cols(chunk)
        y_wait(chunk).wait_recv()
        for k, first in ((1, 0), (3, NZ // 2)):
            part = outs[array].at[x_lo, pl.ds(first, NZ // 2), :, :, where]
            remote(part, part, gx_send.at[chunk], gx_recv.at[chunk], device((x + k) % NX, y, z, core)).start()
        part = outs[array].at[x_lo, :, :, :, where]
        remote(part, part, gs_send.at[chunk], gs_recv.at[chunk], sibling).start()

    def gx_wait(chunk):
        array, where = cols(chunk)
        mine, other = outs[array].at[x_lo, :, :, :, where], outs[array].at[1 - x_lo, :, :, :, where]
        return remote(mine, other, gx_send.at[chunk], gx_recv.at[chunk], sibling)

    def gs_step(chunk):
        array, where = cols(chunk)
        gx_wait(chunk).wait_recv()
        part = outs[array].at[1 - x_lo, :, :, :, where]
        remote(part, part, gs_send.at[chunk], gs_recv.at[chunk], sibling).start()

    def gs_wait(chunk):
        array, first, width = CHUNKS[chunk]
        half = ins[array].shape[1] // 2
        theirs_at = pl.ds(pl.multiple_of((1 - core) * half + first, 128), width)
        _, where = cols(chunk)
        return remote(outs[array].at[:, :, :, :, where], outs[array].at[:, :, :, :, theirs_at], gs_send.at[chunk], gs_recv.at[chunk], sibling)

    floats = tok_ref[0].astype(f32)
    normed[...] = (rms_scaled(floats) * again_ref[...]).astype(bf16)
    lane = lax.broadcasted_iota(jnp.int32, (tokens, experts), 1)
    named = [id_ref[0, :, choice:choice + 1] == lane for choice in range(TOP)]
    either = jnp.where(named[0] | named[1], 1.0, 0.0).astype(bf16)
    down, across = (lax.broadcasted_iota(jnp.int32, (tokens, tokens), i) for i in (0, 1))
    before = jnp.dot(jnp.where(across < down, 1.0, 0.0).astype(bf16), either, preferred_element_type=f32)
    sent_at = []
    for choice in range(TOP):
        slot = jnp.sum(jnp.where(named[choice], before, 0.0), axis=1, keepdims=True).astype(jnp.int32)
        expert = id_ref[0, :, choice:choice + 1]
        chip, low = expert % (NZ * NY), expert // (NZ * NY)
        back_ref[:, choice:choice + 1] = (((chip % NY) * NZ + chip // NY) * 2 + low) * CAP + slot
        place = ((chip * 2 + low) * CAP + slot).astype(f32)
        sent_at.append(jnp.sum(jnp.where(across == down, place, 0.0), axis=0, keepdims=True).astype(jnp.int32))
    row = lax.broadcasted_iota(jnp.int32, (2 * NZ * NY * CAP, tokens), 0)
    chosen_ref[...] = jnp.where((row == sent_at[0]) | (row == sent_at[1]), 1.0, 0.0).astype(bf16)
    loads = [local(src.at[0], dst, w_sem.at[i]) for i, (src, dst) in enumerate(((wg_hbm, wg), (wu_hbm, wu), (wd_hbm, wd)))]

    def matrix(ref, tile):
        return ref[:, :, :, :, tile * TILE:(tile + 1) * TILE].reshape(-1, TILE)

    ctx = (x // 2) * 2 + core
    peers = [device((x + 2) % NX, y, z, core), sibling, device((x + 2) % NX, y, z, 1 - core)]

    def make_keys():
        pair = jnp.dot(normed[...], matrix(kv_all, 0), preferred_element_type=f32)
        key_values[ctx, :, :HD] = rms_scaled(pair[:, :HD]).astype(bf16)
        key_values[ctx, :, HD:] = pair[:, HD:].astype(bf16)
        for peer in peers:
            remote(key_values.at[ctx], key_values.at[ctx], kv_send, kv_recv, peer).start()

    def kv_wait():
        three = key_values.at[pl.ds(0, 3)]
        return remote(three, three, kv_send, kv_recv, sibling)

    def make_queries(tile):
        wide = jnp.dot(normed[...], matrix(q_all, tile), preferred_element_type=f32)
        for head in range(TILE // HD):
            queries[tile * 2 + head] = rms_scaled(wide[:, head * HD:(head + 1) * HD]).astype(bf16)

    def attend(tile):
        keys = key_values[:, :, :HD].reshape(-1, HD)
        values = key_values[:, :, HD:].reshape(-1, HD)
        for head in (tile * 2, tile * 2 + 1):
            scores = lax.dot_general(queries[head], keys, (((1,), (1,)), ((), ())), preferred_element_type=f32) * (HD ** (-0.5))
            weights = jnp.exp(scores).astype(bf16)
            weighted = jnp.dot(weights, values, preferred_element_type=f32)
            totals = jnp.sum(weights.astype(f32), axis=1, keepdims=True)
            context[:, head * HD:(head + 1) * HD] = (weighted / totals).astype(bf16)

    def project(tile):
        att_ref[0, :, tile * TILE:(tile + 1) * TILE] = jnp.dot(context[...], matrix(o_all, tile), preferred_element_type=f32).astype(bf16)

    y_step(0)
    y_step(1)
    x_step(0)
    y_step(2)
    x_step(1)
    gs_step(0)
    gs_wait(0).wait_recv()
    make_keys()
    y_step(3)
    x_step(2)
    gs_step(1)
    gs_wait(1).wait_recv()
    make_queries(0)
    make_queries(2)
    y_step(4)
    x_step(3)
    gs_step(2)
    gs_wait(2).wait_recv()
    make_queries(1)
    make_queries(3)
    kv_wait().wait_recv()
    attend(0)
    x_step(4)
    attend(1)
    gs_step(3)
    attend(2)
    attend(3)
    gs_step(4)
    for load in loads:
        load.start()
    gs_wait(3).wait_recv()
    project(0)
    project(2)
    gs_wait(4).wait_recv()
    project(1)
    project(3)
    mixed = floats + att_ref[0].astype(f32)
    moe_ref[...] = (rms_scaled(mixed) * mgain_ref[...]).astype(bf16)

    sent[...] = jnp.dot(chosen_ref[...], moe_ref[...], preferred_element_type=f32).astype(bf16).reshape(sent.shape)
    for k, d in plane:
        to_z, to_y = (z + k) % NZ, (y + d) % NY
        remote(sent.at[to_z, to_y], came.at[d, z], zy_send, zy_recv.at[d], device(x, to_y, to_z, core)).start()
    own_block = local(sent.at[z, y], came.at[0, z], own_sem.at[0])
    own_block.start()
    logits = jnp.dot(moe_ref[...], router_ref[...], preferred_element_type=f32)
    picked = [jnp.sum(jnp.where(id_ref[0, :, choice:choice + 1] == lane, logits, 0.0), axis=1, keepdims=True) for choice in range(TOP)]
    first = jax.nn.sigmoid(picked[0] - picked[1])
    gate_ref[:, 0:1] = first
    gate_ref[:, 1:2] = 1.0 - first

    def zy_wait(d):
        count = NZ if d else NZ - 1
        return remote(came.at[d, pl.ds(0, count)], came.at[d, pl.ds(0, count)], zy_send, zy_recv.at[d], sibling)

    def spread(d):
        zy_wait(d).wait_recv()
        if d == 0:
            own_block.wait()
        for k, part in ((2, x_lo), (1, 1 - x_lo), (3, 1 - x_lo)):
            remote(came.at[d, :, part], rows.at[d, core, k - 1], x_send.at[d], x_recv.at[d], device((x + k) % NX, y, z, core)).start()
        local(came.at[d, :, x_lo], rows.at[d, core, 3], own_sem.at[1 + d]).start()
        remote(came.at[d, :, x_lo], rows.at[d, core, 3], s_send.at[d], s_recv.at[d], sibling).start()

    def x_wait(d):
        three = rows.at[d, core, pl.ds(0, 3)]
        return remote(three, three, x_send.at[d], x_recv.at[d], sibling)

    def share(d):
        x_wait(d).wait_recv()
        three = rows.at[d, core, pl.ds(0, 3)]
        remote(three, three, s_send.at[d], s_recv.at[d], sibling).start()

    def s_wait(d):
        return remote(rows.at[d, core], rows.at[d, 1 - core], s_send.at[d], s_recv.at[d], sibling)

    def compute(d):
        s_wait(d).wait_recv()
        local(came.at[d, :, x_lo], rows.at[d, core, 3], own_sem.at[1 + d]).wait()
        if d == 0:
            for load in loads:
                load.wait()
        many = rows[d].reshape(2 * NX * block, features)

        def up(tile, carry):
            where = pl.ds(pl.multiple_of(tile * DRAIN, DRAIN), DRAIN)
            gated = jnp.dot(many, wg[:, where], preferred_element_type=f32)
            lifted = jnp.dot(many, wu[:, where], preferred_element_type=f32)
            hidden[:, where] = (gated / (1.0 + jnp.exp(-gated)) * lifted).astype(bf16)
            return carry

        lax.fori_loop(0, wg.shape[1] // DRAIN, up, 0)
        inner = hidden[...]

        def down(tile, carry):
            where = pl.ds(pl.multiple_of(tile * DRAIN, DRAIN), DRAIN)
            term = jnp.dot(inner, wd[:, where], preferred_element_type=f32).astype(bf16)
            terms[d, :, :, :, :, where] = term.reshape(2, NX, NZ, CAP, DRAIN)
            return carry

        lax.fori_loop(0, features // DRAIN, down, 0)
        remote(terms.at[d, 1 - core], theirs.at[d], rs_send.at[d], rs_recv.at[d], sibling).start()

    def rs_wait(d):
        return remote(terms.at[d, 1 - core], theirs.at[d], rs_send.at[d], rs_recv.at[d], sibling)

    def halve(d):
        rs_wait(d).wait_recv()
        halves[d] = (terms[d, core].astype(f32) + theirs[d].astype(f32)).astype(bf16)
        for k in (2, 1, 3):
            remote(halves.at[d, k - 1], sides.at[d, k - 1], rx_send.at[d], rx_recv.at[d], device((x - k + NX) % NX, y, z, core)).start()

    def rx_wait(d):
        return remote(halves.at[d, pl.ds(0, 3)], sides.at[d], rx_send.at[d], rx_recv.at[d], sibling)

    def finish(d):
        rx_wait(d).wait_recv()
        final[d, :, x_lo] = (halves[d, 3].astype(f32) + sides[d, 1].astype(f32)).astype(bf16)
        final[d, :, 1 - x_lo] = (sides[d, 0].astype(f32) + sides[d, 2].astype(f32)).astype(bf16)
        for k in (4, 3, 5, 2, 6, 1, 7, 0):
            if (k, d) == (0, 0):
                local(final.at[d, z], back.at[y, z], own_sem.at[1 + NY]).start()
            else:
                to_z, to_y = (z + k) % NZ, (y - d + NY) % NY
                remote(final.at[d, to_z], back.at[y, z], rz_send, rz_recv.at[d], device(x, to_y, to_z, core)).start()

    def pick(d):
        count, from_y = NZ if d else NZ - 1, (y + d) % NY
        part = back.at[from_y, pl.ds(0, count)]
        remote(part, part, rz_send, rz_recv.at[d], sibling).wait_recv()
        if d == 0:
            local(final.at[d, z], back.at[y, z], own_sem.at[1 + NY]).wait()
        place = lax.broadcasted_iota(jnp.int32, (tokens, 2 * block), 1) + from_y * (2 * block)
        got = back[from_y].reshape(2 * block, features)
        total = None
        for choice in range(TOP):
            mine = jnp.where(place == back_ref[:, choice:choice + 1], 1.0, 0.0).astype(bf16)
            part = gate_ref[:, choice:choice + 1] * jnp.dot(mine, got, preferred_element_type=f32)
            total = part if total is None else total + part
        return total

    spread(0)
    spread(1)
    share(0)
    compute(0)
    spread(3)
    share(1)
    compute(1)
    halve(0)
    spread(2)
    share(3)
    compute(3)
    halve(1)
    finish(0)
    share(2)
    compute(2)
    halve(3)
    finish(1)
    halve(2)
    finish(3)
    finish(2)
    total = pick(0) + pick(1)
    total = total + pick(3)
    total = total + pick(2)
    mix_ref[0] = total.astype(bf16)

    for d in range(NY):
        x_wait(d).wait_send()
        s_wait(d).wait_send()
        rs_wait(d).wait_send()
        rx_wait(d).wait_send()
    for sent_ref, sem in ((came, zy_send), (final, rz_send)):
        some = sent_ref.at[pl.ds(0, NY - 1)]
        remote(some, some, sem, zy_recv.at[0], sibling).wait_send()
        rest = sent_ref.at[0, pl.ds(0, NZ - 1)]
        remote(rest, rest, sem, zy_recv.at[0], sibling).wait_send()
    for chunk in range(len(CHUNKS)):
        z_wait(chunk).wait_send()
        y_wait(chunk).wait_send()
        gx_wait(chunk).wait_send()
        gs_wait(chunk).wait_send()
    kv_wait().wait_send()


def body(
    tokens, expert_ids, attn_gain, w_query, w_kv, w_out, moe_gain, router, w_gate, w_up, w_down
):
    _, rows, features = tokens.shape
    width = w_gate.shape[2]
    heads = w_query.shape[1] // HD
    block = (NZ, CAP, features)
    dma, vmem = pltpu.SemaphoreType.DMA, pltpu.VMEM
    n = len(CHUNKS)
    any_spec, vmem_spec = pl.BlockSpec(memory_space=pl.ANY), pl.BlockSpec(memory_space=vmem)
    return pl.pallas_call(
        layer_kernel,
        out_shape=[jax.ShapeDtypeStruct(tokens.shape, bf16)] * 2,
        in_specs=[vmem_spec] * 5 + [any_spec] * 6,
        out_specs=[vmem_spec] * 2,
        scratch_shapes=[vmem((2, NZ, NY) + w.shape, bf16) for w in (w_query, w_kv, w_out)]
        + [
            vmem((rows, features), bf16),
            vmem((heads, rows, HD), bf16),
            vmem((4, rows, 2 * HD), bf16),
            vmem((rows, heads * HD), bf16),
            vmem((rows, features), bf16),
            vmem((2 * NZ * NY * CAP, rows), bf16),
            vmem((rows, TOP), jnp.int32),
            vmem((rows, TOP), f32),
            vmem((features, width), bf16),
            vmem((features, width), bf16),
            vmem((width, features), bf16),
            vmem((NZ, NY, 2, CAP, features), bf16),
            vmem((NY, NZ, 2, CAP, features), bf16),
            vmem((NY, 2, NX) + block, bf16),
            vmem((2 * NX * NZ * CAP, width), bf16),
            vmem((NY, 2, NX) + block, bf16),
            vmem((NY, NX) + block, bf16),
            vmem((NY, NX) + block, bf16),
            vmem((NY, NX - 1) + block, bf16),
            vmem((NY, NZ, 2, CAP, features), bf16),
            vmem((NY, NZ, 2, CAP, features), bf16),
        ]
        + [dma((n,))] * 9
        + [dma, dma]
        + [
            dma((3,)), dma, dma((NY,)), dma((NY,)), dma((NY,)), dma((NY,)), dma((NY,)), dma((2 + NY,)),
            dma((NY,)), dma((NY,)), dma((NY,)), dma((NY,)), dma, dma((NY,)),
        ],
        compiler_params=pltpu.CompilerParams(collective_id=0, has_side_effects=True, vmem_limit_bytes=60 << 20),
        name="layer",
    )(tokens, expert_ids, attn_gain.reshape(1, -1), moe_gain.reshape(1, -1), router, w_query, w_kv, w_out, w_gate, w_up, w_down)


def solution(mesh):
    in_specs = (
        P("exp", "ctx", None),
        P("exp", "ctx", None),
        P(),
        P("exp", None),
        P("exp", None),
        P("exp", None),
        P(),
        P(),
        P("exp", None, "ctx"),
        P("exp", None, "ctx"),
        P("exp", "ctx", None),
    )
    out_specs = (P("exp", "ctx", None), P("exp", "ctx", None))
    return jax.shard_map(body, mesh=mesh, in_specs=in_specs, out_specs=out_specs, check_vma=False)
```

time: 150 us -> 126 us (0.84)
  blocking collectives: 14.2 us -> 0 us
  matrix products: 4.15 us -> 0 us
  other arithmetic: 3.21 us -> 0 us
    all_gather x2 -> x0, blocking collectives: 14.2 us -> none  [the longest x1 7.25 us: body(): value_piece = lax.all_gather(values, 'ctx', axis=0, tiled=True)]
    unnamed x18 -> x4, local copies, waits for them, and re-layouts: 1.83 us -> 6.5 us
    dot_general x6 -> x0, matrix products: 4.15 us -> none  [the longest x1 1.42 us: body(): key_value = jnp.dot(attn_in, full_kv, preferred_element_type=jnp.float32)]
    dot_general x1 -> x0, local copies, waits for them, and re-layouts: 2.9 us -> none  [body(): jnp.dot(attn_in, full_query, preferred_element_type=jnp.float32)]
    pallas_call x2 -> x1, Pallas kernels: 120 us -> 119 us  [body(): pl.pallas_call(layer_kernel, out_shape=[jax.ShapeDtypeStruct(tokens.shape...]
where the time goes in v3:
time: 126 us
  Pallas kernels  119 us (94%)
  local copies, waits for them, and re-layouts  6.5 us (5%)
    pallas_call x1, Pallas kernels, body(): pl.pallas_call(layer_kernel, out_shape=[jax.ShapeDtypeStruct(tokens.shape...  119 us
    unnamed x4, local copies, waits for them, and re-layouts  6.5 us

profile of v3, /device:TPU:1, one launch (start us, length us, event | category | flops | bytes accessed | tf_op | source)
XLA Modules:
  0.0 126.3 jit_solution(10201017098846707074)
XLA Ops:
  0.6 1.4 %copy.13.id_ref = s32[1,128,2]{2,1,0:T(8,128)} copy(s32[1,128,2]{1,2,0:T(2,128)} %param.12) | data formatting | bytes 2048 | tf_op args[1]
  2.0 1.7 %copy.14.router_ref = bf16[1024,64]{1,0:T(8,128)(2,1)} copy(bf16[1024,64]{0,1:T(8,128)(2,1)} %param.18) | data formatting | bytes 262144 | tf_op args[7]
  3.8 119.1 %layer.1 = (bf16[1,128,1024]{2,1,0:T(8,128)(2,1)}, bf16[1,128,1024]{2,1,0:T(8,128)(2,1)}) custom-call(bf16[1,128,1024]{2,1,0:T(8,128)(2,1)} %tok_ref.1, s32[1,128,2]{2,1,0:T(8,128)} %copy.13.id_ref, f32[1,1024]{1,0:T(1,128)} %bitcast.2, f32[1,1024]{1,0:T(1,128)} %bitcast.3, bf16[1024,64]{1,0:T(8,128)(2,1)} %copy.14.router_ref, bf16[16,1024]{1,0:T(8,128)(2,1)} %q_in.1, ...), custom_call_target="tpu_custom_call" | custom-call | tf_op jit(solution)/shard_map/layer/pallas_call | solution.py:387
  122.9 1.7 %copy.17 = bf16[1,128,1024]{2,1,0:T(8,128)(2,1)} copy(bf16[1,128,1024]{2,1,0:T(8,128)(2,1)} %get-tuple-element.4) | data formatting | bytes 524288
  124.6 1.7 %copy.18 = bf16[1,128,1024]{2,1,0:T(8,128)(2,1)} copy(bf16[1,128,1024]{2,1,0:T(8,128)(2,1)} %get-tuple-element.5) | data formatting | bytes 524288

commit v4 on v3

--- a/solution.py
+++ b/solution.py
@@ -39,6 +39,7 @@
 CHUNKS = ((1, 0, 128), (0, 0, 256), (0, 256, 256), (2, 0, 256), (2, 256, 256))
 TILE = 256
 CAP = 6
+Q, W = 4, 256
 DRAIN = 256
 
 
@@ -51,7 +52,7 @@
 
 
 def layer_kernel(tok_ref, id_ref, again_ref, mgain_ref, router_ref, q_in, kv_in, o_in, wg_hbm, wu_hbm, wd_hbm, att_ref, mix_ref,
-                 q_all, kv_all, o_all, normed, queries, key_values, context, moe_ref, chosen_ref, back_ref, gate_ref,
+                 q_all, kv_all, o_all, normed, queries, key_values, context, moe_ref, quarters, chosen_ref, back_ref, gate_ref, into, outof, many, outcome, mix,
                  wg, wu, wd, sent, came, rows, hidden, terms, theirs, halves, sides, final, back,
                  g_own, z_send, z_recv, y_send, y_recv, gx_send, gx_recv, gs_send, gs_recv, kv_send, kv_recv,
                  w_sem, zy_send, zy_recv, x_send, x_recv, s_send, s_recv, own_sem,
@@ -60,8 +61,9 @@
     x_lo = x % 2
     features = tok_ref.shape[2]
     tokens = tok_ref.shape[1]
-    experts = router_ref.shape[1]
+    experts = router_ref.shape[0]
     block = NZ * CAP
+    high = Q * CAP
     plane = [(k, d) for d in (0, 1, 3, 2) for k in (4, 3, 5, 2, 6, 1, 7, 0) if (k, d) != (0, 0)]
     sibling = device(x, y, z, 1 - core)
     barrier = pltpu.get_barrier_semaphore()
@@ -139,20 +141,25 @@
     floats = tok_ref[0].astype(f32)
     normed[...] = (rms_scaled(floats) * again_ref[...]).astype(bf16)
     lane = lax.broadcasted_iota(jnp.int32, (tokens, experts), 1)
-    named = [id_ref[0, :, choice:choice + 1] == lane for choice in range(TOP)]
+    down, across = (lax.broadcasted_iota(jnp.int32, (tokens, tokens), i) for i in (0, 1))
+    ids = [jnp.sum(jnp.where(across == down, id_ref[0, choice:choice + 1, :].astype(f32), 0.0), axis=1, keepdims=True).astype(jnp.int32) for choice in range(TOP)]
+    named = [ids[choice] == lane for choice in range(TOP)]
     either = jnp.where(named[0] | named[1], 1.0, 0.0).astype(bf16)
-    down, across = (lax.broadcasted_iota(jnp.int32, (tokens, tokens), i) for i in (0, 1))
     before = jnp.dot(jnp.where(across < down, 1.0, 0.0).astype(bf16), either, preferred_element_type=f32)
     sent_at = []
     for choice in range(TOP):
         slot = jnp.sum(jnp.where(named[choice], before, 0.0), axis=1, keepdims=True).astype(jnp.int32)
-        expert = id_ref[0, :, choice:choice + 1]
-        chip, low = expert % (NZ * NY), expert // (NZ * NY)
-        back_ref[:, choice:choice + 1] = (((chip % NY) * NZ + chip // NY) * 2 + low) * CAP + slot
-        place = ((chip * 2 + low) * CAP + slot).astype(f32)
-        sent_at.append(jnp.sum(jnp.where(across == down, place, 0.0), axis=0, keepdims=True).astype(jnp.int32))
-    row = lax.broadcasted_iota(jnp.int32, (2 * NZ * NY * CAP, tokens), 0)
+        chip, low = ids[choice] % (NZ * NY), ids[choice] // (NZ * NY)
+        back_ref[:, choice:choice + 1] = (((chip % NY) * NZ + chip // NY) * 2 + low) * high + slot
+        place = ((chip * 2 + low) * high + slot).astype(f32)
+        place = jnp.sum(jnp.where(across == down, place, 0.0), axis=0, keepdims=True).astype(jnp.int32)
+        sent_at.append(jnp.concatenate([place + q * CAP for q in range(Q)], axis=1))
+    row = lax.broadcasted_iota(jnp.int32, (2 * NZ * NY * high, Q * tokens), 0)
     chosen_ref[...] = jnp.where((row == sent_at[0]) | (row == sent_at[1]), 1.0, 0.0).astype(bf16)
+    for ref, a, b in ((into, 0, 1), (outof, 1, 0)):
+        to, at = (lax.broadcasted_iota(jnp.int32, (NZ * high, NZ * high), i) for i in (a, b))
+        same = (to // block == (at % high) // CAP) & ((to % block) // CAP == at // high) & (to % CAP == at % CAP)
+        ref[...] = jnp.where(same, 1.0, 0.0).astype(bf16)
     loads = [local(src.at[0], dst, w_sem.at[i]) for i, (src, dst) in enumerate(((wg_hbm, wg), (wu_hbm, wu), (wd_hbm, wd)))]
 
     def matrix(ref, tile):
@@ -229,14 +236,16 @@
     mixed = floats + att_ref[0].astype(f32)
     moe_ref[...] = (rms_scaled(mixed) * mgain_ref[...]).astype(bf16)
 
-    sent[...] = jnp.dot(chosen_ref[...], moe_ref[...], preferred_element_type=f32).astype(bf16).reshape(sent.shape)
+    for q in range(Q):
+        quarters[q] = moe_ref[:, q * W:(q + 1) * W]
+    sent[...] = jnp.dot(chosen_ref[...], quarters[...].reshape(Q * tokens, W), preferred_element_type=f32).astype(bf16).reshape(sent.shape)
     for k, d in plane:
         to_z, to_y = (z + k) % NZ, (y + d) % NY
         remote(sent.at[to_z, to_y], came.at[d, z], zy_send, zy_recv.at[d], device(x, to_y, to_z, core)).start()
     own_block = local(sent.at[z, y], came.at[0, z], own_sem.at[0])
     own_block.start()
-    logits = jnp.dot(moe_ref[...], router_ref[...], preferred_element_type=f32)
-    picked = [jnp.sum(jnp.where(id_ref[0, :, choice:choice + 1] == lane, logits, 0.0), axis=1, keepdims=True) for choice in range(TOP)]
+    logits = lax.dot_general(moe_ref[...], router_ref[...], (((1,), (1,)), ((), ())), preferred_element_type=f32)
+    picked = [jnp.sum(jnp.where(named[choice], logits, 0.0), axis=1, keepdims=True) for choice in range(TOP)]
     first = jax.nn.sigmoid(picked[0] - picked[1])
     gate_ref[:, 0:1] = first
     gate_ref[:, 1:2] = 1.0 - first
@@ -272,25 +281,31 @@
         if d == 0:
             for load in loads:
                 load.wait()
-        many = rows[d].reshape(2 * NX * block, features)
+        for group in range(2 * NX):
+            turned = jnp.dot(into[...], rows[d, group // NX, group % NX].reshape(NZ * high, W), preferred_element_type=f32).astype(bf16)
+            for q in range(Q):
+                many[group * block:(group + 1) * block, q * W:(q + 1) * W] = turned[q * block:(q + 1) * block]
 
         def up(tile, carry):
             where = pl.ds(pl.multiple_of(tile * DRAIN, DRAIN), DRAIN)
-            gated = jnp.dot(many, wg[:, where], preferred_element_type=f32)
-            lifted = jnp.dot(many, wu[:, where], preferred_element_type=f32)
+            gated = jnp.dot(many[...], wg[:, where], preferred_element_type=f32)
+            lifted = jnp.dot(many[...], wu[:, where], preferred_element_type=f32)
             hidden[:, where] = (gated / (1.0 + jnp.exp(-gated)) * lifted).astype(bf16)
             return carry
 
         lax.fori_loop(0, wg.shape[1] // DRAIN, up, 0)
         inner = hidden[...]
 
-        def down(tile, carry):
+        def fall(tile, carry):
             where = pl.ds(pl.multiple_of(tile * DRAIN, DRAIN), DRAIN)
-            term = jnp.dot(inner, wd[:, where], preferred_element_type=f32).astype(bf16)
-            terms[d, :, :, :, :, where] = term.reshape(2, NX, NZ, CAP, DRAIN)
+            outcome[:, where] = jnp.dot(inner, wd[:, where], preferred_element_type=f32).astype(bf16)
             return carry
 
-        lax.fori_loop(0, features // DRAIN, down, 0)
+        lax.fori_loop(0, features // DRAIN, fall, 0)
+        for group in range(2 * NX):
+            flat = jnp.concatenate([outcome[group * block:(group + 1) * block, q * W:(q + 1) * W] for q in range(Q)], axis=0)
+            turned = jnp.dot(outof[...], flat, preferred_element_type=f32).astype(bf16)
+            terms[d, group // NX, group % NX] = turned.reshape(NZ, high, W)
         remote(terms.at[d, 1 - core], theirs.at[d], rs_send.at[d], rs_recv.at[d], sibling).start()
 
     def rs_wait(d):
@@ -316,20 +331,24 @@
                 to_z, to_y = (z + k) % NZ, (y - d + NY) % NY
                 remote(final.at[d, to_z], back.at[y, z], rz_send, rz_recv.at[d], device(x, to_y, to_z, core)).start()
 
-    def pick(d):
+    def pick(d, first_pick=False):
         count, from_y = NZ if d else NZ - 1, (y + d) % NY
         part = back.at[from_y, pl.ds(0, count)]
         remote(part, part, rz_send, rz_recv.at[d], sibling).wait_recv()
         if d == 0:
             local(final.at[d, z], back.at[y, z], own_sem.at[1 + NY]).wait()
-        place = lax.broadcasted_iota(jnp.int32, (tokens, 2 * block), 1) + from_y * (2 * block)
-        got = back[from_y].reshape(2 * block, features)
-        total = None
-        for choice in range(TOP):
-            mine = jnp.where(place == back_ref[:, choice:choice + 1], 1.0, 0.0).astype(bf16)
-            part = gate_ref[:, choice:choice + 1] * jnp.dot(mine, got, preferred_element_type=f32)
-            total = part if total is None else total + part
-        return total
+        place = lax.broadcasted_iota(jnp.int32, (tokens, 2 * NZ * high), 1) + from_y * (2 * NZ * high)
+        got = back[from_y].reshape(2 * NZ * high, W)
+        for q in range(Q):
+            total = None
+            for choice in range(TOP):
+                mine = jnp.where(place == back_ref[:, choice:choice + 1] + q * CAP, 1.0, 0.0).astype(bf16)
+                part = gate_ref[:, choice:choice + 1] * jnp.dot(mine, got, preferred_element_type=f32)
+                total = part if total is None else total + part
+            if first_pick:
+                mix[:, q * W:(q + 1) * W] = total
+            else:
+                mix[:, q * W:(q + 1) * W] += total
 
     spread(0)
     spread(1)
@@ -348,13 +367,14 @@
     compute(2)
     halve(3)
     finish(1)
+    pick(0, True)
     halve(2)
     finish(3)
+    pick(1)
     finish(2)
-    total = pick(0) + pick(1)
-    total = total + pick(3)
-    total = total + pick(2)
-    mix_ref[0] = total.astype(bf16)
+    pick(3)
+    pick(2)
+    mix_ref[0] = mix[...].astype(bf16)
 
     for d in range(NY):
         x_wait(d).wait_send()
@@ -374,17 +394,26 @@
     kv_wait().wait_send()
 
 
+def settle(a_ref, b_ref, a_out, b_out, sem):
+    copies = [local(a_ref, a_out, sem.at[0]), local(b_ref, b_out, sem.at[1])]
+    for copy in copies:
+        copy.start()
+    for copy in copies:
+        copy.wait()
+
+
 def body(
     tokens, expert_ids, attn_gain, w_query, w_kv, w_out, moe_gain, router, w_gate, w_up, w_down
 ):
     _, rows, features = tokens.shape
     width = w_gate.shape[2]
     heads = w_query.shape[1] // HD
-    block = (NZ, CAP, features)
+    block = (NZ, Q * CAP, W)
+    piece = (2, Q * CAP, W)
     dma, vmem = pltpu.SemaphoreType.DMA, pltpu.VMEM
     n = len(CHUNKS)
     any_spec, vmem_spec = pl.BlockSpec(memory_space=pl.ANY), pl.BlockSpec(memory_space=vmem)
-    return pl.pallas_call(
+    results = pl.pallas_call(
         layer_kernel,
         out_shape=[jax.ShapeDtypeStruct(tokens.shape, bf16)] * 2,
         in_specs=[vmem_spec] * 5 + [any_spec] * 6,
@@ -396,22 +425,28 @@
             vmem((4, rows, 2 * HD), bf16),
             vmem((rows, heads * HD), bf16),
             vmem((rows, features), bf16),
-            vmem((2 * NZ * NY * CAP, rows), bf16),
+            vmem((Q, rows, W), bf16),
+            vmem((2 * NZ * NY * Q * CAP, Q * rows), bf16),
             vmem((rows, TOP), jnp.int32),
             vmem((rows, TOP), f32),
+            vmem((NZ * Q * CAP, NZ * Q * CAP), bf16),
+            vmem((NZ * Q * CAP, NZ * Q * CAP), bf16),
+            vmem((2 * NX * NZ * CAP, features), bf16),
+            vmem((2 * NX * NZ * CAP, features), bf16),
+            vmem((rows, features), f32),
             vmem((features, width), bf16),
             vmem((features, width), bf16),
             vmem((width, features), bf16),
-            vmem((NZ, NY, 2, CAP, features), bf16),
-            vmem((NY, NZ, 2, CAP, features), bf16),
+            vmem((NZ, NY) + piece, bf16),
+            vmem((NY, NZ) + piece, bf16),
             vmem((NY, 2, NX) + block, bf16),
             vmem((2 * NX * NZ * CAP, width), bf16),
             vmem((NY, 2, NX) + block, bf16),
             vmem((NY, NX) + block, bf16),
             vmem((NY, NX) + block, bf16),
             vmem((NY, NX - 1) + block, bf16),
-            vmem((NY, NZ, 2, CAP, features), bf16),
-            vmem((NY, NZ, 2, CAP, features), bf16),
+            vmem((NY, NZ) + piece, bf16),
+            vmem((NY, NZ) + piece, bf16),
         ]
         + [dma((n,))] * 9
         + [dma, dma]
@@ -421,7 +456,15 @@
         ],
         compiler_params=pltpu.CompilerParams(collective_id=0, has_side_effects=True, vmem_limit_bytes=60 << 20),
         name="layer",
-    )(tokens, expert_ids, attn_gain.reshape(1, -1), moe_gain.reshape(1, -1), router, w_query, w_kv, w_out, w_gate, w_up, w_down)
+    )(tokens, expert_ids.swapaxes(1, 2), attn_gain.reshape(1, -1), moe_gain.reshape(1, -1), router.T, w_query, w_kv, w_out, w_gate, w_up, w_down)
+    return tuple(pl.pallas_call(
+        settle,
+        out_shape=[jax.ShapeDtypeStruct(tokens.shape, bf16)] * 2,
+        in_specs=[any_spec] * 2,
+        out_specs=[any_spec] * 2,
+        scratch_shapes=[dma((2,))],
+        name="settle",
+    )(*results))
 
 
 def solution(mesh):

time: 126 us -> 129 us (1.024)
  Pallas kernels: 119 us -> 128 us
  local copies, waits for them, and re-layouts: 6.5 us -> 0 us
    pallas_call x0 -> x1, Pallas kernels: none -> 17 us  [body(): pl.pallas_call(settle, out_shape=[jax.ShapeDtypeStruct(tokens.shape, bf16...]
    pallas_call x1, Pallas kernels: 119 us -> 111 us  [body(): pl.pallas_call(layer_kernel, out_shape=[jax.ShapeDtypeStruct(tokens.shape...]
    unnamed x4 -> x0, local copies, waits for them, and re-layouts: 6.5 us -> none
where the time goes in v4:
time: 129 us
  Pallas kernels  128 us (99%)
    pallas_call x1, Pallas kernels, body(): pl.pallas_call(layer_kernel, out_shape=[jax.ShapeDtypeStruct(tokens.shape...  111 us
    pallas_call x1, Pallas kernels, body(): pl.pallas_call(settle, out_shape=[jax.ShapeDtypeStruct(tokens.shape, bf16...  17 us

profile of v4, /device:TPU:1, one launch (start us, length us, event | category | flops | bytes accessed | tf_op | source)
XLA Modules:
  0.0 128.7 jit_solution(7482234204732667367)
XLA Ops:
  0.6 110.9 %layer.1 = (bf16[1,128,1024]{2,1,0:T(8,128)(2,1)}, bf16[1,128,1024]{2,1,0:T(8,128)(2,1)}) custom-call(bf16[1,128,1024]{2,1,0:T(8,128)(2,1)} %tok_ref.1, s32[1,2,128]{2,1,0:T(2,128)} %bitcast.7, f32[1,1024]{1,0:T(1,128)} %bitcast.5, f32[1,1024]{1,0:T(1,128)} %bitcast.6, bf16[64,1024]{1,0:T(8,128)(2,1)} %bitcast.4, bf16[16,1024]{1,0:T(8,128)(2,1)} %q_in.1, ...), custom_call_target="tpu_custom_call" | custom-call | tf_op jit(solution)/shard_map/layer/pallas_call | solution.py:416
  111.5 17.0 %settle.1 = (bf16[1,128,1024]{2,1,0:T(8,128)(2,1)}, bf16[1,128,1024]{2,1,0:T(8,128)(2,1)}) custom-call(bf16[1,128,1024]{2,1,0:T(8,128)(2,1)} %get-tuple-element.4.a_ref, bf16[1,128,1024]{2,1,0:T(8,128)(2,1)} %get-tuple-element.5.b_ref), custom_call_target="tpu_custom_call" | custom-call | tf_op jit(solution)/shard_map/settle/pallas_call | solution.py:460

commit v5 on v4

--- a/solution.py
+++ b/solution.py
@@ -40,7 +40,6 @@
 TILE = 256
 CAP = 6
 Q, W = 4, 256
-DRAIN = 256
 
 
 def remote(src, dst, send, recv, target):
@@ -64,10 +63,9 @@
     experts = router_ref.shape[0]
     block = NZ * CAP
     high = Q * CAP
-    plane = [(k, d) for d in (0, 1, 3, 2) for k in (4, 3, 5, 2, 6, 1, 7, 0) if (k, d) != (0, 0)]
     sibling = device(x, y, z, 1 - core)
     barrier = pltpu.get_barrier_semaphore()
-    partners = [device(x, (y + d) % NY, (z + k) % NZ, core) for k, d in plane]
+    partners = [device(x, y, (z + k) % NZ, core) for k in range(1, NZ)] + [device(x, (y + k) % NY, z, core) for k in range(1, NY)]
     partners += [device((x + k) % NX, y, z, core) for k in range(1, NX)]
     partners += [sibling, device((x + 2) % NX, y, z, 1 - core)]
     for partner in partners:
@@ -80,28 +78,29 @@
         half = ins[array].shape[1] // 2
         return array, pl.ds(pl.multiple_of(core * half + first, 128), width)
 
-    own = []
-    for chunk in range(len(CHUNKS)):
-        array, where = cols(chunk)
-        copy = local(ins[array].at[:, where], outs[array].at[x_lo, z, y, :, where], g_own.at[chunk])
-        copy.start()
-        own.append(copy)
+    def span(array):
+        half = ins[array].shape[1] // 2
+        return pl.ds(pl.multiple_of(core * half, 128), half)
+
+    own = {}
+    for array in (1, 0, 2):
+        own[array] = local(ins[array].at[:, span(array)], outs[array].at[x_lo, z, y, :, span(array)], g_own.at[array])
+        own[array].start()
     pl.semaphore_wait(barrier, len(partners))
-    for chunk in range(len(CHUNKS)):
-        array, where = cols(chunk)
+    for array in (1, 0, 2):
         for k in (4, 3, 5, 2, 6, 1, 7):
-            remote(ins[array].at[:, where], outs[array].at[x_lo, z, y, :, where], z_send.at[chunk], z_recv.at[chunk],
+            remote(ins[array].at[:, span(array)], outs[array].at[x_lo, z, y, :, span(array)], z_send.at[array], z_recv.at[array],
                    device(x, y, (z + k) % NZ, core)).start()
 
-    def z_wait(chunk):
-        array, where = cols(chunk)
-        seven = outs[array].at[x_lo, pl.ds(0, NZ - 1), y, :, where]
-        return remote(seven, seven, z_send.at[chunk], z_recv.at[chunk], sibling)
+    def z_wait(array):
+        seven = outs[array].at[x_lo, pl.ds(0, NZ - 1), y, :, span(array)]
+        return remote(seven, seven, z_send.at[array], z_recv.at[array], sibling)
 
     def y_step(chunk):
         array, where = cols(chunk)
-        z_wait(chunk).wait_recv()
-        own[chunk].wait()
+        if CHUNKS[chunk][1] == 0:
+            z_wait(array).wait_recv()
+            own[array].wait()
         part = outs[array].at[x_lo, :, y, :, where]
         for k in (2, 1, 3):
             remote(part, part, y_send.at[chunk], y_recv.at[chunk], device(x, (y + k) % NY, z, core)).start()
@@ -140,26 +139,6 @@
 
     floats = tok_ref[0].astype(f32)
     normed[...] = (rms_scaled(floats) * again_ref[...]).astype(bf16)
-    lane = lax.broadcasted_iota(jnp.int32, (tokens, experts), 1)
-    down, across = (lax.broadcasted_iota(jnp.int32, (tokens, tokens), i) for i in (0, 1))
-    ids = [jnp.sum(jnp.where(across == down, id_ref[0, choice:choice + 1, :].astype(f32), 0.0), axis=1, keepdims=True).astype(jnp.int32) for choice in range(TOP)]
-    named = [ids[choice] == lane for choice in range(TOP)]
-    either = jnp.where(named[0] | named[1], 1.0, 0.0).astype(bf16)
-    before = jnp.dot(jnp.where(across < down, 1.0, 0.0).astype(bf16), either, preferred_element_type=f32)
-    sent_at = []
-    for choice in range(TOP):
-        slot = jnp.sum(jnp.where(named[choice], before, 0.0), axis=1, keepdims=True).astype(jnp.int32)
-        chip, low = ids[choice] % (NZ * NY), ids[choice] // (NZ * NY)
-        back_ref[:, choice:choice + 1] = (((chip % NY) * NZ + chip // NY) * 2 + low) * high + slot
-        place = ((chip * 2 + low) * high + slot).astype(f32)
-        place = jnp.sum(jnp.where(across == down, place, 0.0), axis=0, keepdims=True).astype(jnp.int32)
-        sent_at.append(jnp.concatenate([place + q * CAP for q in range(Q)], axis=1))
-    row = lax.broadcasted_iota(jnp.int32, (2 * NZ * NY * high, Q * tokens), 0)
-    chosen_ref[...] = jnp.where((row == sent_at[0]) | (row == sent_at[1]), 1.0, 0.0).astype(bf16)
-    for ref, a, b in ((into, 0, 1), (outof, 1, 0)):
-        to, at = (lax.broadcasted_iota(jnp.int32, (NZ * high, NZ * high), i) for i in (a, b))
-        same = (to // block == (at % high) // CAP) & ((to % block) // CAP == at // high) & (to % CAP == at % CAP)
-        ref[...] = jnp.where(same, 1.0, 0.0).astype(bf16)
     loads = [local(src.at[0], dst, w_sem.at[i]) for i, (src, dst) in enumerate(((wg_hbm, wg), (wu_hbm, wu), (wd_hbm, wd)))]
 
     def matrix(ref, tile):
@@ -213,6 +192,26 @@
     make_queries(2)
     y_step(4)
     x_step(3)
+    lane = lax.broadcasted_iota(jnp.int32, (tokens, experts), 1)
+    down, across = (lax.broadcasted_iota(jnp.int32, (tokens, tokens), i) for i in (0, 1))
+    ids = [jnp.sum(jnp.where(across == down, id_ref[0, choice:choice + 1, :].astype(f32), 0.0), axis=1, keepdims=True).astype(jnp.int32) for choice in range(TOP)]
+    named = [ids[choice] == lane for choice in range(TOP)]
+    either = jnp.where(named[0] | named[1], 1.0, 0.0).astype(bf16)
+    before = jnp.dot(jnp.where(across < down, 1.0, 0.0).astype(bf16), either, preferred_element_type=f32)
+    sent_at = []
+    for choice in range(TOP):
+        slot = jnp.sum(jnp.where(named[choice], before, 0.0), axis=1, keepdims=True).astype(jnp.int32)
+        chip, low = ids[choice] % (NZ * NY), ids[choice] // (NZ * NY)
+        place = (((chip % NY) * NZ + chip // NY) * 2 + low) * high + slot
+        back_ref[:, choice:choice + 1] = place
+        place = jnp.sum(jnp.where(across == down, place.astype(f32), 0.0), axis=0, keepdims=True).astype(jnp.int32)
+        sent_at.append(jnp.concatenate([place + q * CAP for q in range(Q)], axis=1))
+    row = lax.broadcasted_iota(jnp.int32, (2 * NZ * NY * high, Q * tokens), 0)
+    chosen_ref[...] = jnp.where((row == sent_at[0]) | (row == sent_at[1]), 1.0, 0.0).astype(bf16)
+    for ref, a, b in ((into, 0, 1), (outof, 1, 0)):
+        to, at = (lax.broadcasted_iota(jnp.int32, (NZ * high, NZ * high), i) for i in (a, b))
+        same = (to // block == (at % high) // CAP) & ((to % block) // CAP == at // high) & (to % CAP == at % CAP)
+        ref[...] = jnp.where(same, 1.0, 0.0).astype(bf16)
     gs_step(2)
     gs_wait(2).wait_recv()
     make_queries(1)
@@ -238,11 +237,15 @@
 
     for q in range(Q):
         quarters[q] = moe_ref[:, q * W:(q + 1) * W]
-    sent[...] = jnp.dot(chosen_ref[...], quarters[...].reshape(Q * tokens, W), preferred_element_type=f32).astype(bf16).reshape(sent.shape)
-    for k, d in plane:
-        to_z, to_y = (z + k) % NZ, (y + d) % NY
-        remote(sent.at[to_z, to_y], came.at[d, z], zy_send, zy_recv.at[d], device(x, to_y, to_z, core)).start()
-    own_block = local(sent.at[z, y], came.at[0, z], own_sem.at[0])
+    for d in (0, 1, 3, 2):
+        to_y = (y + d) % NY
+        part = chosen_ref[pl.ds(pl.multiple_of(to_y * (2 * NZ * high), 2 * NZ * high), 2 * NZ * high), :]
+        sent[to_y] = jnp.dot(part, quarters[...].reshape(Q * tokens, W), preferred_element_type=f32).astype(bf16).reshape(NZ, 2, high, W)
+        for k in (4, 3, 5, 2, 6, 1, 7, 0):
+            to_z = (z + k) % NZ
+            if (k, d) != (0, 0):
+                remote(sent.at[to_y, to_z], came.at[d, z], zy_send, zy_recv.at[d], device(x, to_y, to_z, core)).start()
+    own_block = local(sent.at[y, z], came.at[0, z], own_sem.at[0])
     own_block.start()
     logits = lax.dot_general(moe_ref[...], router_ref[...], (((1,), (1,)), ((), ())), preferred_element_type=f32)
     picked = [jnp.sum(jnp.where(named[choice], logits, 0.0), axis=1, keepdims=True) for choice in range(TOP)]
@@ -286,22 +289,10 @@
             for q in range(Q):
                 many[group * block:(group + 1) * block, q * W:(q + 1) * W] = turned[q * block:(q + 1) * block]
 
-        def up(tile, carry):
-            where = pl.ds(pl.multiple_of(tile * DRAIN, DRAIN), DRAIN)
-            gated = jnp.dot(many[...], wg[:, where], preferred_element_type=f32)
-            lifted = jnp.dot(many[...], wu[:, where], preferred_element_type=f32)
-            hidden[:, where] = (gated / (1.0 + jnp.exp(-gated)) * lifted).astype(bf16)
-            return carry
-
-        lax.fori_loop(0, wg.shape[1] // DRAIN, up, 0)
-        inner = hidden[...]
-
-        def fall(tile, carry):
-            where = pl.ds(pl.multiple_of(tile * DRAIN, DRAIN), DRAIN)
-            outcome[:, where] = jnp.dot(inner, wd[:, where], preferred_element_type=f32).astype(bf16)
-            return carry
-
-        lax.fori_loop(0, features // DRAIN, fall, 0)
+        gated = jnp.dot(many[...], wg[...], preferred_element_type=f32)
+        lifted = jnp.dot(many[...], wu[...], preferred_element_type=f32)
+        hidden[...] = (gated / (1.0 + jnp.exp(-gated)) * lifted).astype(bf16)
+        outcome[...] = jnp.dot(hidden[...], wd[...], preferred_element_type=f32).astype(bf16)
         for group in range(2 * NX):
             flat = jnp.concatenate([outcome[group * block:(group + 1) * block, q * W:(q + 1) * W] for q in range(Q)], axis=0)
             turned = jnp.dot(outof[...], flat, preferred_element_type=f32).astype(bf16)
@@ -386,20 +377,18 @@
         remote(some, some, sem, zy_recv.at[0], sibling).wait_send()
         rest = sent_ref.at[0, pl.ds(0, NZ - 1)]
         remote(rest, rest, sem, zy_recv.at[0], sibling).wait_send()
+    for array in range(3):
+        z_wait(array).wait_send()
     for chunk in range(len(CHUNKS)):
-        z_wait(chunk).wait_send()
         y_wait(chunk).wait_send()
         gx_wait(chunk).wait_send()
         gs_wait(chunk).wait_send()
     kv_wait().wait_send()
 
 
-def settle(a_ref, b_ref, a_out, b_out, sem):
-    copies = [local(a_ref, a_out, sem.at[0]), local(b_ref, b_out, sem.at[1])]
-    for copy in copies:
-        copy.start()
-    for copy in copies:
-        copy.wait()
+def settle(a_ref, b_ref, a_out, b_out):
+    a_out[...] = a_ref[...]
+    b_out[...] = b_ref[...]
 
 
 def body(
@@ -437,7 +426,7 @@
             vmem((features, width), bf16),
             vmem((features, width), bf16),
             vmem((width, features), bf16),
-            vmem((NZ, NY) + piece, bf16),
+            vmem((NY, NZ) + piece, bf16),
             vmem((NY, NZ) + piece, bf16),
             vmem((NY, 2, NX) + block, bf16),
             vmem((2 * NX * NZ * CAP, width), bf16),
@@ -460,9 +449,8 @@
     return tuple(pl.pallas_call(
         settle,
         out_shape=[jax.ShapeDtypeStruct(tokens.shape, bf16)] * 2,
-        in_specs=[any_spec] * 2,
-        out_specs=[any_spec] * 2,
-        scratch_shapes=[dma((2,))],
+        in_specs=[vmem_spec] * 2,
+        out_specs=[vmem_spec] * 2,
         name="settle",
     )(*results))
 

time: 129 us -> 107 us (0.83)
  Pallas kernels: 128 us -> 106 us
    pallas_call x1, Pallas kernels: 17 us -> 1.84 us  [body(): pl.pallas_call(settle, out_shape=[jax.ShapeDtypeStruct(tokens.shape, bf16...]
    pallas_call x1, Pallas kernels: 111 us -> 104 us  [body(): pl.pallas_call(layer_kernel, out_shape=[jax.ShapeDtypeStruct(tokens.shape...]
where the time goes in v5:
time: 107 us
  Pallas kernels  106 us (99%)
    pallas_call x1, Pallas kernels, body(): pl.pallas_call(layer_kernel, out_shape=[jax.ShapeDtypeStruct(tokens.shape...  104 us

profile of v5, /device:TPU:1, one launch (start us, length us, event | category | flops | bytes accessed | tf_op | source)
XLA Modules:
  0.0 107.0 jit_solution(5789448540380263855)
XLA Ops:
  0.6 104.5 %layer.1 = (bf16[1,128,1024]{2,1,0:T(8,128)(2,1)}, bf16[1,128,1024]{2,1,0:T(8,128)(2,1)}) custom-call(bf16[1,128,1024]{2,1,0:T(8,128)(2,1)} %tok_ref.1, s32[1,2,128]{2,1,0:T(2,128)} %bitcast.7, f32[1,1024]{1,0:T(1,128)} %bitcast.5, f32[1,1024]{1,0:T(1,128)} %bitcast.6, bf16[64,1024]{1,0:T(8,128)(2,1)} %bitcast.4, bf16[16,1024]{1,0:T(8,128)(2,1)} %q_in.1, ...), custom_call_target="tpu_custom_call" | custom-call | tf_op jit(solution)/shard_map/layer/pallas_call | solution.py:405
  105.1 1.8 %settle.1 = (bf16[1,128,1024]{2,1,0:T(8,128)(2,1)}, bf16[1,128,1024]{2,1,0:T(8,128)(2,1)}) custom-call(bf16[1,128,1024]{2,1,0:T(8,128)(2,1)} %get-tuple-element.4.a_ref, bf16[1,128,1024]{2,1,0:T(8,128)(2,1)} %get-tuple-element.5.b_ref), custom_call_target="tpu_custom_call" | custom-call | tf_op jit(solution)/shard_map/settle/pallas_call | solution.py:449

commit v6 on v5

--- a/solution.py
+++ b/solution.py
@@ -78,29 +78,28 @@
         half = ins[array].shape[1] // 2
         return array, pl.ds(pl.multiple_of(core * half + first, 128), width)
 
-    def span(array):
-        half = ins[array].shape[1] // 2
-        return pl.ds(pl.multiple_of(core * half, 128), half)
-
-    own = {}
-    for array in (1, 0, 2):
-        own[array] = local(ins[array].at[:, span(array)], outs[array].at[x_lo, z, y, :, span(array)], g_own.at[array])
-        own[array].start()
+    own = []
+    for chunk in range(len(CHUNKS)):
+        array, where = cols(chunk)
+        copy = local(ins[array].at[:, where], outs[array].at[x_lo, z, y, :, where], g_own.at[chunk])
+        copy.start()
+        own.append(copy)
     pl.semaphore_wait(barrier, len(partners))
-    for array in (1, 0, 2):
+    for chunk in range(len(CHUNKS)):
+        array, where = cols(chunk)
         for k in (4, 3, 5, 2, 6, 1, 7):
-            remote(ins[array].at[:, span(array)], outs[array].at[x_lo, z, y, :, span(array)], z_send.at[array], z_recv.at[array],
+            remote(ins[array].at[:, where], outs[array].at[x_lo, z, y, :, where], z_send.at[chunk], z_recv.at[chunk],
                    device(x, y, (z + k) % NZ, core)).start()
 
-    def z_wait(array):
-        seven = outs[array].at[x_lo, pl.ds(0, NZ - 1), y, :, span(array)]
-        return remote(seven, seven, z_send.at[array], z_recv.at[array], sibling)
+    def z_wait(chunk):
+        array, where = cols(chunk)
+        seven = outs[array].at[x_lo, pl.ds(0, NZ - 1), y, :, where]
+        return remote(seven, seven, z_send.at[chunk], z_recv.at[chunk], sibling)
 
     def y_step(chunk):
         array, where = cols(chunk)
-        if CHUNKS[chunk][1] == 0:
-            z_wait(array).wait_recv()
-            own[array].wait()
+        z_wait(chunk).wait_recv()
+        own[chunk].wait()
         part = outs[array].at[x_lo, :, y, :, where]
         for k in (2, 1, 3):
             remote(part, part, y_send.at[chunk], y_recv.at[chunk], device(x, (y + k) % NY, z, core)).start()
@@ -235,16 +234,23 @@
     mixed = floats + att_ref[0].astype(f32)
     moe_ref[...] = (rms_scaled(mixed) * mgain_ref[...]).astype(bf16)
 
+    def half_at(part):
+        return ((z // (NZ // 2) + 1 + part) % 2) * (NZ // 2)
+
+    def half_of(part):
+        return pl.ds(half_at(part), NZ // 2)
+
     for q in range(Q):
         quarters[q] = moe_ref[:, q * W:(q + 1) * W]
     for d in (0, 1, 3, 2):
         to_y = (y + d) % NY
         part = chosen_ref[pl.ds(pl.multiple_of(to_y * (2 * NZ * high), 2 * NZ * high), 2 * NZ * high), :]
         sent[to_y] = jnp.dot(part, quarters[...].reshape(Q * tokens, W), preferred_element_type=f32).astype(bf16).reshape(NZ, 2, high, W)
-        for k in (4, 3, 5, 2, 6, 1, 7, 0):
-            to_z = (z + k) % NZ
-            if (k, d) != (0, 0):
-                remote(sent.at[to_y, to_z], came.at[d, z], zy_send, zy_recv.at[d], device(x, to_y, to_z, core)).start()
+        for part in range(2):
+            for k in (3, 1, 2, 0):
+                to_z = half_at(part) + (z + k) % (NZ // 2)
+                if (k, d, part) != (0, 0, 1):
+                    remote(sent.at[to_y, to_z], came.at[d, z], zy_send, zy_recv.at[d, part], device(x, to_y, to_z, core)).start()
     own_block = local(sent.at[y, z], came.at[0, z], own_sem.at[0])
     own_block.start()
     logits = lax.dot_general(moe_ref[...], router_ref[...], (((1,), (1,)), ((), ())), preferred_element_type=f32)
@@ -253,26 +259,25 @@
     gate_ref[:, 0:1] = first
     gate_ref[:, 1:2] = 1.0 - first
 
-    def zy_wait(d):
-        count = NZ if d else NZ - 1
-        return remote(came.at[d, pl.ds(0, count)], came.at[d, pl.ds(0, count)], zy_send, zy_recv.at[d], sibling)
-
-    def spread(d):
-        zy_wait(d).wait_recv()
-        if d == 0:
+    def spread(d, part):
+        where, count = half_of(part), NZ // 2 - (1 if (d, part) == (0, 1) else 0)
+        some = came.at[d, pl.ds(half_at(part), count)]
+        remote(some, some, zy_send, zy_recv.at[d, part], sibling).wait_recv()
+        if (d, part) == (0, 1):
             own_block.wait()
-        for k, part in ((2, x_lo), (1, 1 - x_lo), (3, 1 - x_lo)):
-            remote(came.at[d, :, part], rows.at[d, core, k - 1], x_send.at[d], x_recv.at[d], device((x + k) % NX, y, z, core)).start()
-        local(came.at[d, :, x_lo], rows.at[d, core, 3], own_sem.at[1 + d]).start()
-        remote(came.at[d, :, x_lo], rows.at[d, core, 3], s_send.at[d], s_recv.at[d], sibling).start()
+        for k, low in ((2, x_lo), (1, 1 - x_lo), (3, 1 - x_lo)):
+            remote(came.at[d, where, low], rows.at[d, core, k - 1, where], x_send.at[d], x_recv.at[d, part], device((x + k) % NX, y, z, core)).start()
+        if part == 1:
+            local(came.at[d, :, x_lo], rows.at[d, core, 3], own_sem.at[1 + d]).start()
+            remote(came.at[d, :, x_lo], rows.at[d, core, 3], s_send.at[d], s_recv.at[d], sibling).start()
 
     def x_wait(d):
         three = rows.at[d, core, pl.ds(0, 3)]
-        return remote(three, three, x_send.at[d], x_recv.at[d], sibling)
-
-    def share(d):
-        x_wait(d).wait_recv()
-        three = rows.at[d, core, pl.ds(0, 3)]
+        return remote(three, three, x_send.at[d], x_recv.at[d, 0], sibling)
+
+    def share(d, part):
+        three = rows.at[d, core, pl.ds(0, 3), half_of(part)]
+        remote(three, three, x_send.at[d], x_recv.at[d, part], sibling).wait_recv()
         remote(three, three, s_send.at[d], s_recv.at[d], sibling).start()
 
     def s_wait(d):
@@ -305,22 +310,27 @@
     def halve(d):
         rs_wait(d).wait_recv()
         halves[d] = (terms[d, core].astype(f32) + theirs[d].astype(f32)).astype(bf16)
-        for k in (2, 1, 3):
-            remote(halves.at[d, k - 1], sides.at[d, k - 1], rx_send.at[d], rx_recv.at[d], device((x - k + NX) % NX, y, z, core)).start()
+        for part in range(2):
+            where = half_of(part)
+            for k in (2, 1, 3):
+                remote(halves.at[d, k - 1, where], sides.at[d, k - 1, where], rx_send.at[d], rx_recv.at[d, part], device((x - k + NX) % NX, y, z, core)).start()
 
     def rx_wait(d):
-        return remote(halves.at[d, pl.ds(0, 3)], sides.at[d], rx_send.at[d], rx_recv.at[d], sibling)
+        return remote(halves.at[d, pl.ds(0, 3)], sides.at[d], rx_send.at[d], rx_recv.at[d, 0], sibling)
 
     def finish(d):
-        rx_wait(d).wait_recv()
-        final[d, :, x_lo] = (halves[d, 3].astype(f32) + sides[d, 1].astype(f32)).astype(bf16)
-        final[d, :, 1 - x_lo] = (sides[d, 0].astype(f32) + sides[d, 2].astype(f32)).astype(bf16)
-        for k in (4, 3, 5, 2, 6, 1, 7, 0):
-            if (k, d) == (0, 0):
-                local(final.at[d, z], back.at[y, z], own_sem.at[1 + NY]).start()
-            else:
-                to_z, to_y = (z + k) % NZ, (y - d + NY) % NY
-                remote(final.at[d, to_z], back.at[y, z], rz_send, rz_recv.at[d], device(x, to_y, to_z, core)).start()
+        for part in range(2):
+            where = half_of(part)
+            three = sides.at[d, :, where]
+            remote(three, three, rx_send.at[d], rx_recv.at[d, part], sibling).wait_recv()
+            final[d, where, x_lo] = (halves[d, 3, where].astype(f32) + sides[d, 1, where].astype(f32)).astype(bf16)
+            final[d, where, 1 - x_lo] = (sides[d, 0, where].astype(f32) + sides[d, 2, where].astype(f32)).astype(bf16)
+            for k in (3, 1, 2, 0):
+                to_z, to_y = half_at(part) + (z + k) % (NZ // 2), (y - d + NY) % NY
+                if (k, d, part) == (0, 0, 1):
+                    local(final.at[d, z], back.at[y, z], own_sem.at[1 + NY]).start()
+                else:
+                    remote(final.at[d, to_z], back.at[y, z], rz_send, rz_recv.at[d], device(x, to_y, to_z, core)).start()
 
     def pick(d, first_pick=False):
         count, from_y = NZ if d else NZ - 1, (y + d) % NY
@@ -341,23 +351,31 @@
             else:
                 mix[:, q * W:(q + 1) * W] += total
 
-    spread(0)
-    spread(1)
-    share(0)
+    spread(0, 0)
+    spread(0, 1)
+    share(0, 0)
+    spread(1, 0)
+    share(0, 1)
+    spread(1, 1)
     compute(0)
-    spread(3)
-    share(1)
+    share(1, 0)
+    spread(3, 0)
+    share(1, 1)
+    halve(0)
+    spread(3, 1)
     compute(1)
-    halve(0)
-    spread(2)
-    share(3)
+    share(3, 0)
+    spread(2, 0)
+    share(3, 1)
+    halve(1)
+    spread(2, 1)
+    finish(0)
     compute(3)
-    halve(1)
-    finish(0)
-    share(2)
-    compute(2)
+    share(2, 0)
+    share(2, 1)
     halve(3)
     finish(1)
+    compute(2)
     pick(0, True)
     halve(2)
     finish(3)
@@ -374,12 +392,11 @@
         rx_wait(d).wait_send()
     for sent_ref, sem in ((came, zy_send), (final, rz_send)):
         some = sent_ref.at[pl.ds(0, NY - 1)]
-        remote(some, some, sem, zy_recv.at[0], sibling).wait_send()
+        remote(some, some, sem, rz_recv.at[0], sibling).wait_send()
         rest = sent_ref.at[0, pl.ds(0, NZ - 1)]
-        remote(rest, rest, sem, zy_recv.at[0], sibling).wait_send()
-    for array in range(3):
-        z_wait(array).wait_send()
+        remote(rest, rest, sem, rz_recv.at[0], sibling).wait_send()
     for chunk in range(len(CHUNKS)):
+        z_wait(chunk).wait_send()
         y_wait(chunk).wait_send()
         gx_wait(chunk).wait_send()
         gs_wait(chunk).wait_send()
@@ -440,8 +457,8 @@
         + [dma((n,))] * 9
         + [dma, dma]
         + [
-            dma((3,)), dma, dma((NY,)), dma((NY,)), dma((NY,)), dma((NY,)), dma((NY,)), dma((2 + NY,)),
-            dma((NY,)), dma((NY,)), dma((NY,)), dma((NY,)), dma, dma((NY,)),
+            dma((3,)), dma, dma((NY, 2)), dma((NY,)), dma((NY, 2)), dma((NY,)), dma((NY,)), dma((2 + NY,)),
+            dma((NY,)), dma((NY,)), dma((NY,)), dma((NY, 2)), dma, dma((NY,)),
         ],
         compiler_params=pltpu.CompilerParams(collective_id=0, has_side_effects=True, vmem_limit_bytes=60 << 20),
         name="layer",

time: 107 us -> 103 us (0.963)
  Pallas kernels: 106 us -> 102 us
    pallas_call x1, Pallas kernels: 104 us -> 100 us  [body(): pl.pallas_call(layer_kernel, out_shape=[jax.ShapeDtypeStruct(tokens.shape...]
where the time goes in v6:
time: 103 us
  Pallas kernels  102 us (99%)
    pallas_call x1, Pallas kernels, body(): pl.pallas_call(layer_kernel, out_shape=[jax.ShapeDtypeStruct(tokens.shape...  100 us

profile of v6, /device:TPU:1, one launch (start us, length us, event | category | flops | bytes accessed | tf_op | source)
XLA Modules:
  0.0 102.8 jit_solution(16691234244305379494)
XLA Ops:
  0.6 100.4 %layer.1 = (bf16[1,128,1024]{2,1,0:T(8,128)(2,1)}, bf16[1,128,1024]{2,1,0:T(8,128)(2,1)}) custom-call(bf16[1,128,1024]{2,1,0:T(8,128)(2,1)} %tok_ref.1, s32[1,2,128]{2,1,0:T(2,128)} %bitcast.7, f32[1,1024]{1,0:T(1,128)} %bitcast.5, f32[1,1024]{1,0:T(1,128)} %bitcast.6, bf16[64,1024]{1,0:T(8,128)(2,1)} %bitcast.4, bf16[16,1024]{1,0:T(8,128)(2,1)} %q_in.1, ...), custom_call_target="tpu_custom_call" | custom-call | tf_op jit(solution)/shard_map/layer/pallas_call | solution.py:422
  101.0 1.8 %settle.1 = (bf16[1,128,1024]{2,1,0:T(8,128)(2,1)}, bf16[1,128,1024]{2,1,0:T(8,128)(2,1)}) custom-call(bf16[1,128,1024]{2,1,0:T(8,128)(2,1)} %get-tuple-element.4.a_ref, bf16[1,128,1024]{2,1,0:T(8,128)(2,1)} %get-tuple-element.5.b_ref), custom_call_target="tpu_custom_call" | custom-call | tf_op jit(solution)/shard_map/settle/pallas_call | solution.py:466

commit v7 on v6

--- a/solution.py
+++ b/solution.py
@@ -215,9 +215,9 @@
     gs_wait(2).wait_recv()
     make_queries(1)
     make_queries(3)
+    x_step(4)
     kv_wait().wait_recv()
     attend(0)
-    x_step(4)
     attend(1)
     gs_step(3)
     attend(2)
@@ -242,7 +242,7 @@
 
     for q in range(Q):
         quarters[q] = moe_ref[:, q * W:(q + 1) * W]
-    for d in (0, 1, 3, 2):
+    for d in (1, 2, 3, 0):
         to_y = (y + d) % NY
         part = chosen_ref[pl.ds(pl.multiple_of(to_y * (2 * NZ * high), 2 * NZ * high), 2 * NZ * high), :]
         sent[to_y] = jnp.dot(part, quarters[...].reshape(Q * tokens, W), preferred_element_type=f32).astype(bf16).reshape(NZ, 2, high, W)
@@ -286,7 +286,7 @@
     def compute(d):
         s_wait(d).wait_recv()
         local(came.at[d, :, x_lo], rows.at[d, core, 3], own_sem.at[1 + d]).wait()
-        if d == 0:
+        if d == 1:
             for load in loads:
                 load.wait()
         for group in range(2 * NX):
@@ -351,38 +351,38 @@
             else:
                 mix[:, q * W:(q + 1) * W] += total
 
+    spread(1, 0)
+    spread(1, 1)
+    share(1, 0)
+    spread(2, 0)
+    share(1, 1)
+    spread(2, 1)
+    compute(1)
+    share(2, 0)
+    spread(3, 0)
+    share(2, 1)
+    halve(1)
+    spread(3, 1)
+    compute(2)
+    share(3, 0)
     spread(0, 0)
+    share(3, 1)
+    halve(2)
     spread(0, 1)
+    finish(1)
+    compute(3)
     share(0, 0)
-    spread(1, 0)
     share(0, 1)
-    spread(1, 1)
+    halve(3)
+    finish(2)
     compute(0)
-    share(1, 0)
-    spread(3, 0)
-    share(1, 1)
+    pick(1, True)
     halve(0)
-    spread(3, 1)
-    compute(1)
-    share(3, 0)
-    spread(2, 0)
-    share(3, 1)
-    halve(1)
-    spread(2, 1)
+    finish(3)
+    pick(2)
     finish(0)
-    compute(3)
-    share(2, 0)
-    share(2, 1)
-    halve(3)
-    finish(1)
-    compute(2)
-    pick(0, True)
-    halve(2)
-    finish(3)
-    pick(1)
-    finish(2)
     pick(3)
-    pick(2)
+    pick(0)
     mix_ref[0] = mix[...].astype(bf16)
 
     for d in range(NY):

time: 103 us -> 102 us (level)
  no operation moved by 1% of the time
where the time goes in v7:
time: 102 us
  Pallas kernels  102 us (100%)
    pallas_call x1, Pallas kernels, body(): pl.pallas_call(layer_kernel, out_shape=[jax.ShapeDtypeStruct(tokens.shape...  99.9 us

profile of v7, /device:TPU:1, one launch (start us, length us, event | category | flops | bytes accessed | tf_op | source)
XLA Modules:
  0.0 102.4 jit_solution(14995594760504038786)
XLA Ops:
  0.6 99.9 %layer.1 = (bf16[1,128,1024]{2,1,0:T(8,128)(2,1)}, bf16[1,128,1024]{2,1,0:T(8,128)(2,1)}) custom-call(bf16[1,128,1024]{2,1,0:T(8,128)(2,1)} %tok_ref.1, s32[1,2,128]{2,1,0:T(2,128)} %bitcast.7, f32[1,1024]{1,0:T(1,128)} %bitcast.5, f32[1,1024]{1,0:T(1,128)} %bitcast.6, bf16[64,1024]{1,0:T(8,128)(2,1)} %bitcast.4, bf16[16,1024]{1,0:T(8,128)(2,1)} %q_in.1, ...), custom_call_target="tpu_custom_call" | custom-call | tf_op jit(solution)/shard_map/layer/pallas_call | solution.py:422
  100.5 1.8 %settle.1 = (bf16[1,128,1024]{2,1,0:T(8,128)(2,1)}, bf16[1,128,1024]{2,1,0:T(8,128)(2,1)}) custom-call(bf16[1,128,1024]{2,1,0:T(8,128)(2,1)} %get-tuple-element.4.a_ref, bf16[1,128,1024]{2,1,0:T(8,128)(2,1)} %get-tuple-element.5.b_ref), custom_call_target="tpu_custom_call" | custom-call | tf_op jit(solution)/shard_map/settle/pallas_call | solution.py:466
